TPU v7x, 128 devices: a whole 4x4x4 slice. The times are simulated.
128 devices in a mesh: gossip: 4 (over x_hi, core), field: 32 (over x_lo, z, y).
Axes of the slice: x: 4 (x_hi: 2, x_lo: 2; x = x_hi * 2 + x_lo), y: 4, z: 4, core: 2. Of those that a mesh axis runs over, the one named last changes fastest.
Arguments:
- measured_features: bfloat16 [8, 128, 96, 512], P('gossip', 'field'), may hold values from -6 to 6
- feeder_of_row: int32 [128], P('field'), may hold values from 0 to 127, each once
- feeder_table: bfloat16 [128, 512], replicated, may hold values from -3 to 3
- time_qkv: bfloat16 [512, 1536], replicated, may hold values from -0.25 to 0.25
- time_out: bfloat16 [512, 512], replicated, may hold values from -0.25 to 0.25
- feed_qkv: bfloat16 [512, 1536], replicated, may hold values from -0.25 to 0.25
- feed_out: bfloat16 [512, 512], replicated, may hold values from -0.25 to 0.25
- adjoint_of_prediction: bfloat16 [8, 128, 96, 512], P('gossip', None, 'field'), may hold values from -0.09375 to 0.09375
- round_index: int32 [1], replicated, may hold values from 0 to 1
Outputs:
- predicted_load: bfloat16 [8, 128, 96, 512], P('gossip', None, 'field')
- peer_mean_derivatives: float32 [4, 4096, 512], P('gossip')
All inputs are finite; a program needn't handle non-finite values.
Results may differ from a plain program's by a relative error of at most 0.02.
Values may be sent and summed in bfloat16 or wider, within the bound.
A program may use at most 128 MiB of HBM per device.

v0:
```python
from functools import partial
import math

import jax
import jax.numpy as jnp
from jax import lax
from jax.sharding import PartitionSpec as P

HEADS = 8


epsilon = 1e-05


def normalize(hidden):
    wide = hidden.astype(jnp.float32)
    factor = lax.rsqrt(jnp.mean(wide * wide, axis=-1, keepdims=True) + epsilon)
    return (wide * factor).astype(jnp.bfloat16)


def attend(stacked_array, heads, causal):
    groups, length, triple = stacked_array.shape
    width = triple // 3
    size = width // heads
    parts = stacked_array.reshape(groups, length, 3, heads, size)
    query = parts[:, :, 0]
    keys = parts[:, :, 1]
    values = parts[:, :, 2]
    scores = jnp.einsum("glhe,gmhe->ghlm", query, keys, preferred_element_type=jnp.float32) * (
        1.0 / math.sqrt(size)
    )
    powers = jnp.exp(scores)
    if causal:
        allowed = jnp.arange(length)[:, None] >= jnp.arange(length)[None, :]
        powers = jnp.where(allowed, powers, 0.0)
    shares = powers / jnp.sum(powers, axis=-1, keepdims=True)
    rounded = shares.astype(jnp.bfloat16)
    mixed_slope_estimate = jnp.einsum(
        "ghlm,gmhe->glhe", rounded, values, preferred_element_type=jnp.float32
    )
    return mixed_slope_estimate.reshape(groups, length, width).astype(jnp.bfloat16)


def sublayer_forward(hidden, w_qkv, w_out, heads, causal):
    groups, length, width = hidden.shape
    normed, norm_back = jax.vjp(normalize, hidden)
    stacked_array = jnp.dot(normed.reshape(-1, width), w_qkv, preferred_element_type=jnp.float32)
    stacked_array = stacked_array.astype(jnp.bfloat16).reshape(groups, length, 3 * width)
    mixed_slope_estimate, attend_back = jax.vjp(
        partial(attend, heads=heads, causal=causal), stacked_array
    )
    result = hidden.astype(jnp.float32) + jnp.dot(
        mixed_slope_estimate.reshape(-1, width), w_out, preferred_element_type=jnp.float32
    ).reshape(groups, length, width)
    return (result, (normed, mixed_slope_estimate, norm_back, attend_back))


def sublayer_backward(upstream, saved, w_qkv, w_out, need_input):
    normed, mixed_slope_estimate, norm_back, attend_back = saved
    groups, length, width = upstream.shape
    flat_up = upstream.reshape(-1, width)
    grad_out = jnp.dot(
        mixed_slope_estimate.reshape(-1, width).T, flat_up, preferred_element_type=jnp.float32
    )
    grad_mixed = (
        jnp.dot(flat_up, w_out.T, preferred_element_type=jnp.float32)
        .astype(jnp.bfloat16)
        .reshape(groups, length, width)
    )
    (grad_packed,) = attend_back(grad_mixed)
    flat_packed = grad_packed.reshape(-1, 3 * width)
    grad_qkv = jnp.dot(normed.reshape(-1, width).T, flat_packed, preferred_element_type=jnp.float32)
    if not need_input:
        return (grad_qkv, grad_out, None)
    grad_normed = (
        jnp.dot(flat_packed, w_qkv.T, preferred_element_type=jnp.float32)
        .astype(jnp.bfloat16)
        .reshape(groups, length, width)
    )
    (grad_hidden,) = norm_back(grad_normed)
    combined = (grad_hidden.astype(jnp.float32) + upstream.astype(jnp.float32)).astype(jnp.bfloat16)
    return (grad_qkv, grad_out, combined)


def embed(rows, feeder_table):
    table_rows = feeder_table.shape[0]
    onehot = (rows[:, None] == jnp.arange(table_rows, dtype=jnp.int32)[None, :]).astype(
        jnp.bfloat16
    )
    return jnp.dot(onehot, feeder_table, preferred_element_type=jnp.float32)


def on_device(
    measured_features,
    feeder_of_row,
    feeder_table,
    time_qkv,
    time_out,
    feed_qkv,
    feed_out,
    adjoint_of_prediction,
    round_index,
):
    batch, feed_local, slot_count, width = measured_features.shape
    feeder_count = adjoint_of_prediction.shape[1]
    slot_local = adjoint_of_prediction.shape[2]
    added = embed(feeder_of_row, feeder_table)
    start = measured_features.astype(jnp.float32) + added[None, :, None, :]
    start = start.reshape(batch * feed_local, slot_count, width)
    first, saved_time = sublayer_forward(start, time_qkv, time_out, HEADS, True)
    first = first.astype(jnp.bfloat16).reshape(batch, feed_local, slot_count, width)
    by_slot = lax.all_to_all(first, "field", split_axis=2, concat_axis=1, tiled=True)
    regrouped = jnp.transpose(by_slot, (0, 2, 1, 3)).reshape(
        batch * slot_local, feeder_count, width
    )
    right_factor, saved_feed = sublayer_forward(regrouped, feed_qkv, feed_out, HEADS, False)
    right_factor = right_factor.astype(jnp.bfloat16).reshape(batch, slot_local, feeder_count, width)
    predicted_load = jnp.transpose(right_factor, (0, 2, 1, 3))
    upstream = jnp.transpose(adjoint_of_prediction, (0, 2, 1, 3)).reshape(
        batch * slot_local, feeder_count, width
    )
    feeder_query_gradient, grad_fo, regrouped_gradient_rows = sublayer_backward(
        upstream, saved_feed, feed_qkv, feed_out, True
    )
    grad_slots = jnp.transpose(
        regrouped_gradient_rows.reshape(batch, slot_local, feeder_count, width), (0, 2, 1, 3)
    )
    grad_first = lax.all_to_all(grad_slots, "field", split_axis=1, concat_axis=2, tiled=True)
    grad_first = grad_first.reshape(batch * feed_local, slot_count, width)
    grad_tq, grad_to, unused = sublayer_backward(grad_first, saved_time, time_qkv, time_out, False)
    local_grads = jnp.concatenate(
        [grad_tq.reshape(-1, width), grad_to, feeder_query_gradient.reshape(-1, width), grad_fo],
        axis=0,
    )
    partner = jnp.bitwise_xor(
        lax.axis_index("gossip"), jnp.left_shift(jnp.int32(1), round_index[0])
    )
    summed = lax.psum(local_grads.astype(jnp.bfloat16), "field")
    every = lax.all_gather(summed[None], "gossip", axis=0, tiled=True)
    other = lax.dynamic_index_in_dim(every, partner, 0, keepdims=False)
    mixed_slope_estimate = (summed.astype(jnp.float32) + other.astype(jnp.float32)) * 0.5
    return (predicted_load, mixed_slope_estimate[None])


def solution(mesh):
    placed = (
        P("gossip", "field", None, None),
        P("field"),
        P(),
        P(),
        P(),
        P(),
        P(),
        P("gossip", None, "field", None),
        P(),
    )
    return jax.shard_map(
        on_device,
        mesh=mesh,
        in_specs=placed,
        out_specs=(P("gossip", None, "field", None), P("gossip", None, None)),
        check_vma=False,
    )
```

profile of v0, /device:TPU:0, one launch (start us, length us, event | category | flops | bytes accessed | tf_op | source)
XLA Modules:
  0.0 618.6 jit_solution(7549897967458397493)
XLA Ops:
  9.9 2.2 multiply_convert_fusion
  12.3 4.2 convolution_convert_fusion.1
  16.6 6.9 %reshape.195 = bf16[8,96,3,8,64]{4,3,2,1,0:T(8,128)(2,1)} reshape(bf16[768,1536]{1,0:T(8,128)(2,1)} %convolution_convert_fusion.1) | data formatting | bytes 4718592 | tf_op jit(solution)/shard_map/jvp()/reshape;reshape | solution.py:25
  23.5 4.6 fusion.71
  28.1 2.7 copy.318
  30.8 2.7 copy.319
  33.5 2.7 copy.320
  36.2 2.6 fusion.17
  42.3 1.5 copy.266
  43.8 9.7 %all-to-all-start = ((bf16[2,4,96,512]{3,1,0,2:T(4,128)(2,1)}), bf16[2,4,96,512]{3,1,0,2:T(4,128)(2,1)}, u32[]{:S(2)}, u32[]{:S(2)}) async-start(bf16[2,4,96,512]{3,1,0,2:T(4,128)(2,1)} %copy.266), calls=%async_computation | async-start | bytes 1572864 | tf_op jit(solution)/shard_map/all_to_all | solution.py:112
  53.5 2.6 convolution_convert_fusion.14
  57.6 1.9 reshape.176
  59.5 1.7 copy.300
  61.1 2.8 convert_element_type.247
  63.9 3.8 all-to-all-done
  71.6 1.5 copy.270
  73.1 1.6 fusion.23
  74.7 2.8 convolution_convert_fusion
  77.5 6.9 %reshape.196 = bf16[6,128,3,8,64]{4,3,2,1,0:T(8,128)(2,1)} reshape(bf16[768,1536]{1,0:T(8,128)(2,1)} %convolution_convert_fusion) | data formatting | bytes 4718592 | tf_op jit(solution)/shard_map/jvp()/reshape;reshape | solution.py:25
  84.5 4.7 fusion.70
  89.1 2.7 copy.321
  91.8 2.6 copy.322
  94.4 3.1 copy.323
  97.5 2.3 fusion.18
  105.6 2.1 copy.286
  107.7 1.4 fusion.29
  109.8 1.5 fusion.47
  111.3 1.7 copy.291
  113.0 4.7 all-to-all-start.1
  117.7 1.8 convolution_convert_fusion.15
  119.6 1.6 copy.301
  121.1 2.6 convolution_convert_fusion.2
  123.7 1.6 reshape.181
  125.4 2.9 convolution_convert_fusion.16
  128.2 3.1 all-to-all-done.1
  132.5 2.9 convolution_convert_fusion.12
  135.4 2.3 copy.293
  137.7 2.4 reshape.178
  142.0 2.7 fusion.12
  148.8 4.5 copy.299
  153.4 6.1 reshape.179
  159.4 4.2 convolution_convert_fusion.3
  163.7 3.8 reshape.180
  167.5 3.3 pad_maximum_fusion
  170.9 320.3 %all-reduce.8.cloned.1.call-done = bf16[4096,512]{1,0:T(8,128)(2,1)} async-done(((bf16[4096,512]{1,0:T(8,128)(2,1)}), bf16[4096,512]{1,0:T(8,128)(2,1)}) %all-reduce.8.cloned.1.call-update) | async-done | bytes 4194320 | tf_op jit(solution)/shard_map/psum | solution.py:138
  491.9 1.5 fusion.24
  493.4 109.8 %all-gather.3.cloned.1.call-done = bf16[16384,512]{1,0:T(8,128)(2,1)} async-done(((bf16[4096,512]{1,0:T(8,128)(2,1)}), bf16[16384,512]{1,0:T(8,128)(2,1)}) %all-gather.3.cloned.1.call-update) | async-done | bytes 16777232 | tf_op jit(solution)/shard_map/all_gather | solution.py:139
  603.2 8.4 %fusion.1 = f32[1,4096,512]{2,1,0:T(8,128)} fusion(bf16[4096,512]{1,0:T(8,128)(2,1)} %all-reduce.8.cloned.1.call-done, bf16[4,4096,512]{2,1,0:T(8,128)(2,1)} %bitcast.212, s32[]{:T(128)S(6)} %select_n.14), kind=kLoop, calls=%fused_computation.2 | loop fusion | flops 8388608 | bytes 16777220 | tf_op jit(solution)/shard_map/broadcast_in_dim | solution.py:142
  (100 shorter events, 25.2 us)
Async XLA Ops:
  7.2 67.5 %copy-start = (bf16[512,1536]{1,0:T(8,128)(2,1)S(1)}, bf16[512,1536]{1,0:T(8,128)(2,1)}, u32[]{:S(2)}) copy-start(bf16[512,1536]{1,0:T(8,128)(2,1)} %param.14) | copy-start | bytes 4718596
  38.7 2.6 copy-start.5
  38.7 2.0 copy-start.12
  38.8 2.6 copy-start.27
  40.8 1.2 copy-start.3
  41.3 1.0 copy-start.7
  42.0 11.6 %copy-start.21 = (bf16[2,128,3,512]{3,1,2,0:T(8,128)(2,1)S(1)}, bf16[2,128,3,512]{3,1,2,0:T(8,128)(2,1)}, u32[]{:S(2)}) copy-start(bf16[2,128,3,512]{3,1,2,0:T(8,128)(2,1)} %param.16) | copy-start | bytes 2359300
  43.8 23.9 %all-to-all-start = ((bf16[2,4,96,512]{3,1,0,2:T(4,128)(2,1)}), bf16[2,4,96,512]{3,1,0,2:T(4,128)(2,1)}, u32[]{:S(2)}, u32[]{:S(2)}) async-start(bf16[2,4,96,512]{3,1,0,2:T(4,128)(2,1)} %copy.266), calls=%async_computation | async-start | bytes 1572864 | tf_op jit(solution)/shard_map/all_to_all | solution.py:112
  53.5 5.9 copy-start.8
  97.5 2.3 copy-start.15
  97.5 2.3 copy-start.20
  99.9 1.4 copy-start.17
  101.3 3.0 copy-start.10
  101.3 1.7 copy-start.16
  107.7 1.7 copy-start.18
  107.7 2.0 copy-start.22
  109.8 8.0 %copy-start.11 = (bf16[6,8,128,128]{2,3,1,0:T(8,128)(2,1)S(1)}, bf16[6,8,128,128]{2,3,1,0:T(8,128)(2,1)}, u32[]{:S(2)}) copy-start(bf16[6,8,128,128]{2,3,1,0:T(8,128)(2,1)} %copy-done.10) | copy-start | bytes 4718596
  113.0 18.4 %all-to-all-start.1 = ((bf16[2,128,3,512]{3,0,2,1:T(2,128)(2,1)}), bf16[2,128,3,512]{3,0,2,1:T(2,128)(2,1)S(1)}, u32[]{:S(2)}, u32[]{:S(2)}) async-start(bf16[2,128,3,512]{3,0,2,1:T(2,128)(2,1)} %copy.291), calls=%async_computation.1 | async-start | bytes 1572864 | tf_op jit(solution)/shard_map/all_to_all | solution.py:128
  117.7 373.5 %all-reduce.8.cloned.1.call-start = ((), (), s32[]{:S(2)}) async-start(), calls=%async_computation.2 | async-start | bytes 8388608 | tf_op jit(solution)/shard_map/psum | solution.py:138
  117.7 3.4 copy-start.19
  132.5 2.9 copy-start.24
  132.5 7.6 %copy-start.4 = (bf16[8,8,96,96]{2,3,1,0:T(8,128)(2,1)S(1)}, bf16[8,8,96,96]{2,3,1,0:T(8,128)(2,1)}, u32[]{:S(2)}) copy-start(bf16[8,8,96,96]{2,3,1,0:T(8,128)(2,1)} %copy-done.3) | copy-start | bytes 3538948
  140.1 1.9 copy-start.6
  142.0 2.7 copy-start.14
  144.7 1.2 copy-start.13
  146.0 1.4 copy-start.23
  146.0 1.4 copy-start.25
  153.4 6.1 copy-start.26
  163.7 3.9 copy-start.9
  163.7 3.9 copy-start.29
  170.8 321.0 %copy-start.2 = (f32[2,128,3,512]{3,1,2,0:T(8,128)S(1)}, f32[2,128,3,512]{3,1,2,0:T(8,128)}, u32[]{:S(2)}) copy-start(f32[2,128,3,512]{3,1,2,0:T(8,128)} %copy.270) | copy-start | bytes 4718596
  170.9 321.0 %copy-start.28 = (bf16[512,512]{1,0:T(8,128)(2,1)S(1)}, bf16[512,512]{1,0:T(8,128)(2,1)}, u32[]{:S(2)}) copy-start(bf16[512,512]{1,0:T(8,128)(2,1)} %param.15) | copy-start | bytes 1572868
  170.9 432.3 %all-gather.3.cloned.1.call-start = ((), (), s32[]{:S(2)}) async-start(), calls=%async_computation.3 | async-start | bytes 20971520 | tf_op jit(solution)/shard_map/all_gather | solution.py:139
  603.2 8.4 %copy-start.1 = (bf16[512,1536]{1,0:T(8,128)(2,1)S(1)}, bf16[512,1536]{1,0:T(8,128)(2,1)}, u32[]{:S(2)}) copy-start(bf16[512,1536]{1,0:T(8,128)(2,1)} %param.14) | copy-start | bytes 4718596
Sparse Core Ops, SparseCore 0:
  171.0 320.1 all-reduce.7
  492.9 110.2 all-gather.2
where the time goes:
time: 627 us; the launch traced here: 619 us
  waiting for transfers between devices  437 us (70%)
  local copies, waits for them, and re-layouts  83.3 us (13%)
  matrix products  45.9 us (7%)
  other arithmetic  22.3 us (4%)
  between operations  15.5 us (2%)
  starting transfers between devices  14.5 us (2%)
    psum x1, waiting for transfers between devices, on_device(): summed = lax.psum(local_grads.astype(jnp.bfloat16), 'field')  320 us
    all_gather x1, waiting for transfers between devices, on_device(): every = lax.all_gather(summed[None], 'gossip', axis=0, tiled=True)  110 us
    unnamed x66, local copies, waits for them, and re-layouts  19.9 us
    another operation x2, local copies, waits for them, and re-layouts, attend(): parts = stacked_array.reshape(groups, length, 3, heads, size)  13.9 us
  transfers between devices with their start and end apart: 4, of which 4 were waited for; matrix products, arithmetic and copies ran while one was open for 4% of the time, Pallas kernels for 0%

commit v1 on v0

--- a/solution.py
+++ b/solution.py
@@ -4,6 +4,8 @@
 import jax
 import jax.numpy as jnp
 from jax import lax
+from jax.experimental import pallas as pl
+from jax.experimental.pallas import tpu as pltpu
 from jax.sharding import PartitionSpec as P
 
 HEADS = 8
@@ -88,6 +90,180 @@
         jnp.bfloat16
     )
     return jnp.dot(onehot, feeder_table, preferred_element_type=jnp.float32)
+
+
+MESH = pl.DeviceIdType.MESH
+LANES = 128
+UNIT = 1024
+
+
+def coordinates():
+    gossip = lax.axis_index("gossip")
+    field = lax.axis_index("field")
+    x_hi, core = gossip // 2, gossip % 2
+    x_lo, z, y = field // 16, (field // 4) % 4, field % 4
+
+    def at(x_hi, core, x_lo, z, y):
+        return (x_hi * 2 + core, (x_lo * 4 + z) * 4 + y)
+
+    def even(position):
+        return position + 1 - 2 * (position % 2)
+
+    return {
+        "ya": (((y + 1) // 2) % 2, at(x_hi, core, x_lo, z, even(y))),
+        "yb": (y // 2, at(x_hi, core, x_lo, z, 3 - y)),
+        "za": (((z + 1) // 2) % 2, at(x_hi, core, x_lo, even(z), y)),
+        "zb": (z // 2, at(x_hi, core, x_lo, 3 - z, y)),
+        "xa": ((x_hi + x_lo) % 2, at(x_hi, core, 1 - x_lo, z, y)),
+        "xb": (x_hi, at(1 - x_hi, core, 1 - x_lo, z, y)),
+        "core": (core, at(x_hi, 1 - core, x_lo, z, y)),
+    }
+
+
+def block_of(rows):
+    for parts in range(1, rows + 1):
+        if rows % parts == 0 and rows // parts <= 256 and (rows // parts) % 16 == 0:
+            return rows // parts
+    return rows
+
+
+def reduce_kernel(chains, used, g_ref, out_ref, acc, full, inbox, rs_send, rs_recv, ag_send, ag_recv, out_sem):
+    links = coordinates()
+    barrier = pltpu.get_barrier_semaphore()
+    for name in used:
+        pl.semaphore_signal(barrier, inc=1, device_id=links[name][1], device_id_type=MESH)
+    pl.semaphore_wait(barrier, len(used))
+
+    steps = len(used)
+    state = []
+    for start, wave, order in chains:
+        state.append({"at": [start], "start": start})
+
+    def halves(j, s):
+        start, wave, order = chains[j]
+        bit, peer = links[order[s]]
+        rows = UNIT >> (s + 1)
+        base = state[j]["at"][s]
+        return base + bit * rows, base + (1 - bit) * rows, rows, peer
+
+    def rs_copy(j, s):
+        keep, leave, rows, peer = halves(j, s)
+        source = g_ref if s == 0 else acc
+        slot = chains[j][0] + UNIT - 2 * rows
+        return pltpu.make_async_remote_copy(
+            src_ref=source.at[pl.ds(pl.multiple_of(leave, 16), rows)],
+            dst_ref=inbox.at[pl.ds(slot, rows)],
+            send_sem=rs_send.at[j, s],
+            recv_sem=rs_recv.at[j, s],
+            device_id=peer,
+            device_id_type=MESH,
+        )
+
+    def rs_add(j, s):
+        keep, leave, rows, peer = halves(j, s)
+        slot = chains[j][0] + UNIT - 2 * rows
+        source = g_ref if s == 0 else acc
+        target = full if s == steps - 1 else acc
+        block = block_of(rows)
+
+        def add(i, carry):
+            here = pl.ds(pl.multiple_of(keep + i * block, 16), block)
+            there = pl.ds(pl.multiple_of(slot + i * block, 16), block)
+            total = source[here, :].astype(jnp.float32) + inbox[there, :].astype(jnp.float32)
+            if s == steps - 1:
+                total = total * 0.5
+            target[here, :] = total.astype(jnp.bfloat16)
+            return carry
+
+        lax.fori_loop(0, rows // block, add, 0)
+        state[j]["at"].append(keep)
+
+    def ag_copy(j, s):
+        keep, leave, rows, peer = halves(j, s)
+        mine = full.at[pl.ds(pl.multiple_of(keep, 16), rows)]
+        return pltpu.make_async_remote_copy(
+            src_ref=mine,
+            dst_ref=mine,
+            send_sem=ag_send.at[j, s],
+            recv_sem=ag_recv.at[j, s],
+            device_id=peer,
+            device_id_type=MESH,
+        )
+
+    for j in range(len(chains)):
+        rs_copy(j, 0).start()
+    waves = 1 + max(chain[1] for chain in chains)
+    for turn in range(2 * steps + waves - 1):
+        for wave in range(waves):
+            stage = turn - wave
+            if not 0 <= stage < 2 * steps:
+                continue
+            for j in range(len(chains)):
+                if chains[j][1] != wave:
+                    continue
+                if stage < steps:
+                    rs_copy(j, stage).wait()
+                    rs_add(j, stage)
+                    if stage + 1 < steps:
+                        rs_copy(j, stage + 1).start()
+                    else:
+                        ag_copy(j, steps - 1).start()
+                else:
+                    s = 2 * steps - 1 - stage
+                    ag_copy(j, s).wait()
+                    if s > 0:
+                        ag_copy(j, s - 1).start()
+                    else:
+                        part = pl.ds(chains[j][0], UNIT)
+                        pltpu.make_async_copy(full.at[part], out_ref.at[part], out_sem.at[j]).start()
+    for j in range(len(chains)):
+        part = pl.ds(chains[j][0], UNIT)
+        pltpu.make_async_copy(full.at[part], out_ref.at[part], out_sem.at[j]).wait()
+
+
+def reduce_over(first, links, collective_id):
+    used = tuple(first) + tuple(links)
+
+    def run(g):
+        rows = g.shape[0]
+        count = rows // UNIT
+        chains = []
+        for j in range(count):
+            turn = j % len(links)
+            order = tuple(first) + tuple(links[(turn + s) % len(links)] for s in range(len(links)))
+            chains.append((j * UNIT, j // len(links), order))
+        steps = len(used)
+        return pl.pallas_call(
+            partial(reduce_kernel, tuple(chains), used),
+            out_shape=jax.ShapeDtypeStruct(g.shape, jnp.bfloat16),
+            in_specs=[pl.BlockSpec(memory_space=pltpu.VMEM)],
+            out_specs=pl.BlockSpec(memory_space=pl.ANY),
+            scratch_shapes=[
+                pltpu.VMEM(g.shape, jnp.bfloat16),
+                pltpu.VMEM(g.shape, jnp.bfloat16),
+                pltpu.VMEM(g.shape, jnp.bfloat16),
+                pltpu.SemaphoreType.DMA((count, steps)),
+                pltpu.SemaphoreType.DMA((count, steps)),
+                pltpu.SemaphoreType.DMA((count, steps)),
+                pltpu.SemaphoreType.DMA((count, steps)),
+                pltpu.SemaphoreType.DMA((count,)),
+            ],
+            compiler_params=pltpu.CompilerParams(
+                collective_id=collective_id, has_side_effects=True, vmem_limit_bytes=40 << 20
+            ),
+        )(g)
+
+    return run
+
+
+def pair_mean(g, round_index):
+    links = ("ya", "za", "xa", "yb", "zb")
+    return lax.cond(
+        round_index[0] == 0,
+        reduce_over(("core",), links, 1),
+        reduce_over((), links + ("xb",), 2),
+        g,
+    )
 
 
 def on_device(
@@ -132,14 +308,10 @@
         [grad_tq.reshape(-1, width), grad_to, feeder_query_gradient.reshape(-1, width), grad_fo],
         axis=0,
     )
-    partner = jnp.bitwise_xor(
-        lax.axis_index("gossip"), jnp.left_shift(jnp.int32(1), round_index[0])
-    )
-    summed = lax.psum(local_grads.astype(jnp.bfloat16), "field")
-    every = lax.all_gather(summed[None], "gossip", axis=0, tiled=True)
-    other = lax.dynamic_index_in_dim(every, partner, 0, keepdims=False)
-    mixed_slope_estimate = (summed.astype(jnp.float32) + other.astype(jnp.float32)) * 0.5
-    return (predicted_load, mixed_slope_estimate[None])
+    tiles = local_grads.astype(jnp.bfloat16).reshape(512, 8, 4, LANES).transpose(0, 2, 1, 3).reshape(-1, LANES)
+    mean = pair_mean(tiles, round_index)
+    mean = mean.reshape(512, 4, 8, LANES).transpose(0, 2, 1, 3).reshape(4096, 512).astype(jnp.float32)
+    return (predicted_load, mean[None])
 
 
 def solution(mesh):

time: 627 us -> 239 us (0.38); the launches traced: 619 us -> 237 us
  waiting for transfers between devices: 437 us -> 4.39 us
  Pallas kernels: 0 us -> 67.5 us
  between operations: 15.5 us -> 2.2 us
    psum x1 -> x0, waiting for transfers between devices: 320 us -> none  [on_device(): summed = lax.psum(local_grads.astype(jnp.bfloat16), 'field')]
    all_gather x1 -> x0, waiting for transfers between devices: 110 us -> none  [on_device(): every = lax.all_gather(summed[None], 'gossip', axis=0, tiled=True)]
    pallas_call x0 -> x1, Pallas kernels: none -> 67.5 us  [run(): pl.pallas_call(partial(reduce_kernel, tuple(chains), used), out_shape=jax...]
    broadcast_in_dim x1 -> x0, other arithmetic: 8.35 us -> none  [on_device(): return (predicted_load, mixed_slope_estimate[None])]
    convert_element_type x0 -> x1, other arithmetic: none -> 6.9 us  [on_device(): mean.reshape(512, 4, 8, LANES).transpose(0, 2, 1, 3).reshape(4096, 512)]
    unnamed x66 -> x58, local copies, waits for them, and re-layouts: 19.9 us -> 19.7 us
  transfers between devices with their start and end apart: 4 -> 2, of which waited for: 4 -> 2; matrix products, arithmetic and copies ran while one was open for 4% -> 10% of each run, Pallas kernels for 0% -> 0%
where the time goes in v1:
time: 239 us; the launch traced here: 237 us
  local copies, waits for them, and re-layouts  82.1 us (34%)
  Pallas kernels  67.5 us (28%)
  matrix products  47.8 us (20%)
  other arithmetic  18 us (8%)
  starting transfers between devices  15 us (6%)
  waiting for transfers between devices  4.39 us (2%)
    pallas_call x1, Pallas kernels, run(): pl.pallas_call(partial(reduce_kernel, tuple(chains), used), out_shape=jax...  67.5 us
    unnamed x58, local copies, waits for them, and re-layouts  19.7 us
    another operation x2, local copies, waits for them, and re-layouts, attend(): parts = stacked_array.reshape(groups, length, 3, heads, size)  13.9 us
    dot_general x6, matrix products, attend(): jnp.einsum('glhe,gmhe->ghlm', query, keys, preferred_element_type=jnp.flo...  9.8 us
    all_to_all x1, starting transfers between devices, on_device(): lax.all_to_all(first, 'field', split_axis=2, concat_axis=1, tiled=True)  9.66 us
    slice x2, local copies, waits for them, and re-layouts, attend(): values = parts[:, :, 2]  9.24 us
    dot_general x6, matrix products, attend(): jnp.einsum('ghlm,gmhe->glhe', rounded, values, preferred_element_type=jnp...  8.41 us
    dot_general x2, matrix products, sublayer_forward(): jnp.dot(normed.reshape(-1, width), w_qkv, preferred_element_type=jnp.floa...  7.07 us
  transfers between devices with their start and end apart: 2, of which 2 were waited for; matrix products, arithmetic and copies ran while one was open for 10% of the time, Pallas kernels for 0%

profile of v1, /device:TPU:0, one launch (start us, length us, event | category | flops | bytes accessed | tf_op | source)
XLA Modules:
  0.0 237.0 jit_solution(8707470149374542230)
XLA Ops:
  1.9 1.4 multiply_reduce_fusion
  3.4 2.2 multiply_convert_fusion
  5.8 4.2 %convolution_convert_fusion.1 = bf16[768,1536]{1,0:T(8,128)(2,1)} fusion(bf16[768,512]{1,0:T(8,128)(2,1)S(1)} %fusion.25, bf16[512,1536]{1,0:T(8,128)(2,1)} %param.14), kind=kOutput, calls=%fused_computation.7 | convolution fusion | flops 1209139200 | bytes 4718592 | tf_op jit(solution)/shard_map/dot_general | solution.py:49
  10.0 6.9 %reshape.225 = bf16[8,96,3,8,64]{4,3,2,1,0:T(8,128)(2,1)} reshape(bf16[768,1536]{1,0:T(8,128)(2,1)} %convolution_convert_fusion.1) | data formatting | bytes 4718592 | tf_op jit(solution)/shard_map/jvp()/reshape;reshape | solution.py:27
  17.0 4.6 %fusion.69 = (bf16[8,96,1,8,64]{4,3,2,1,0:T(8,128)(2,1)}, bf16[8,96,1,8,64]{4,3,2,1,0:T(8,128)(2,1)}, bf16[8,96,1,8,64]{4,3,2,1,0:T(8,128)(2,1)}) fusion(bf16[8,96,3,8,64]{4,3,2,1,0:T(8,128)(2,1)} %reshape.225), kind=kLoop, calls=%fused_computation.116 | loop fusion | bytes 4718592 | tf_op jit(solution)/shard_map/jvp()/slice | solution.py:30
  21.6 2.7 %copy.318 = bf16[8,96,1,8,64]{1,4,3,0,2:T(8,128)(2,1)} copy(bf16[8,96,1,8,64]{4,3,2,1,0:T(8,128)(2,1)} %get-tuple-element.10) | data formatting | bytes 1572864
  24.2 2.7 %copy.319 = bf16[8,96,1,8,64]{1,4,3,0,2:T(8,128)(2,1)} copy(bf16[8,96,1,8,64]{4,3,2,1,0:T(8,128)(2,1)} %get-tuple-element.11) | data formatting | bytes 1572864
  27.0 2.7 %copy.320 = bf16[8,96,1,8,64]{1,4,3,0,2:T(8,128)(2,1)} copy(bf16[8,96,1,8,64]{4,3,2,1,0:T(8,128)(2,1)} %get-tuple-element.12) | data formatting | bytes 1572864
  29.7 2.6 %fusion.15 = (f32[8,8,96]{2,1,0:T(8,128)S(1)}, f32[8,8,96,96]{2,3,1,0:T(8,128)S(1)}) fusion(pred[96,96]{0,1:T(8,128)(4,1)S(1)} %iota_compare_fusion, bf16[8,96,1,8,64]{1,4,3,0,2:T(8,128)(2,1)} %copy.320, bf16[8,96,1,8,64]{1,4,3,0,2:T(8,128)(2,1)} %copy.319), kind=kOutput, calls=%fused_computation.32 | convolution fusion | flops 77260800 | bytes 3965952 | tf_op jit(solution)/shard_map/jvp(glhe,gmhe->ghlm)/dot_general | solution.py:31
  35.8 1.5 copy.266
  37.3 9.7 %all-to-all-start = ((bf16[2,4,96,512]{3,1,0,2:T(4,128)(2,1)}), bf16[2,4,96,512]{3,1,0,2:T(4,128)(2,1)}, u32[]{:S(2)}, u32[]{:S(2)}) async-start(bf16[2,4,96,512]{3,1,0,2:T(4,128)(2,1)} %copy.266), calls=%async_computation | async-start | bytes 1572864 | tf_op jit(solution)/shard_map/all_to_all | solution.py:288
  47.7 2.5 %convolution_convert_fusion.14 = bf16[768,512]{1,0:T(8,128)(2,1)} fusion(bf16[768,512]{1,0:T(8,128)(2,1)S(1)} %bitcast.222, bf16[512,512]{1,0:T(8,128)(2,1)} %param.17), kind=kOutput, calls=%fused_computation.68 | convolution fusion | flops 403046400 | bytes 2097152 | tf_op jit(solution)/shard_map/dot_general | solution.py:68
  50.3 1.4 copy.280
  51.7 1.9 reshape.204
  53.6 1.7 copy.300
  55.3 2.7 %convert_element_type.269 = bf16[768,512]{0,1:T(8,128)(2,1)} reshape(bf16[8,96,8,64]{1,0,3,2:T(8,128)(2,1)} %copy.300) | data formatting | bytes 1572864 | tf_op jit(solution)/shard_map/jvp()/convert_element_type | solution.py:43
  58.0 3.1 %all-to-all-done = bf16[2,4,96,512]{3,1,0,2:T(4,128)(2,1)} async-done(((bf16[2,4,96,512]{3,1,0,2:T(4,128)(2,1)}), bf16[2,4,96,512]{3,1,0,2:T(4,128)(2,1)}, u32[]{:S(2)}, u32[]{:S(2)}) %all-to-all-start) | async-done | bytes 786464 | tf_op jit(solution)/shard_map/all_to_all | solution.py:288
  61.2 1.4 copy_convert_fusion
  65.1 1.5 copy.270
  66.6 1.6 fusion.21
  68.2 2.8 %convolution_convert_fusion = bf16[768,1536]{1,0:T(8,128)(2,1)} fusion(bf16[768,512]{1,0:T(8,128)(2,1)S(1)} %fusion.21, bf16[512,1536]{1,0:T(8,128)(2,1)S(1)} %copy-done), kind=kOutput, calls=%fused_computation.6 | convolution fusion | flops 1209139200 | bytes 4718592 | tf_op jit(solution)/shard_map/dot_general | solution.py:49
  71.1 6.9 %reshape.226 = bf16[6,128,3,8,64]{4,3,2,1,0:T(8,128)(2,1)} reshape(bf16[768,1536]{1,0:T(8,128)(2,1)} %convolution_convert_fusion) | data formatting | bytes 4718592 | tf_op jit(solution)/shard_map/jvp()/reshape;reshape | solution.py:27
  78.0 4.7 %fusion.68 = (bf16[6,128,1,8,64]{4,3,2,1,0:T(8,128)(2,1)}, bf16[6,128,1,8,64]{4,3,2,1,0:T(8,128)(2,1)}, bf16[6,128,1,8,64]{4,3,2,1,0:T(8,128)(2,1)}) fusion(bf16[6,128,3,8,64]{4,3,2,1,0:T(8,128)(2,1)} %reshape.226), kind=kLoop, calls=%fused_computation.115 | loop fusion | bytes 4718592 | tf_op jit(solution)/shard_map/jvp()/slice | solution.py:30
  82.7 2.7 %copy.321 = bf16[6,128,1,8,64]{1,4,3,0,2:T(8,128)(2,1)} copy(bf16[6,128,1,8,64]{4,3,2,1,0:T(8,128)(2,1)} %get-tuple-element.7) | data formatting | bytes 1572864
  85.3 2.6 %copy.322 = bf16[6,128,1,8,64]{1,4,3,0,2:T(8,128)(2,1)} copy(bf16[6,128,1,8,64]{4,3,2,1,0:T(8,128)(2,1)} %get-tuple-element.8) | data formatting | bytes 1572864
  88.0 3.0 %copy.323 = bf16[6,128,1,8,64]{1,4,3,0,2:T(8,128)(2,1)} copy(bf16[6,128,1,8,64]{4,3,2,1,0:T(8,128)(2,1)} %get-tuple-element.9) | data formatting | bytes 1572864
  91.0 2.3 fusion.16
  99.1 2.1 copy.286
  101.2 1.4 fusion.27
  103.6 1.7 copy.291
  105.3 2.8 %convolution_convert_fusion.2 = bf16[512,1536]{1,0:T(8,128)(2,1)} fusion(bf16[768,512]{1,0:T(8,128)(2,1)S(1)} %bitcast.224, bf16[192,8,6,128]{3,2,1,0:T(8,128)(2,1)S(1)} %bitcast.218), kind=kOutput, calls=%fused_computation.24 | convolution fusion | flops 1208745984 | bytes 4718592 | tf_op jit(solution)/shard_map/dot_general | solution.py:74
  108.1 5.3 %all-to-all-start.1 = ((bf16[2,128,3,512]{3,0,2,1:T(2,128)(2,1)}), bf16[2,128,3,512]{3,0,2,1:T(2,128)(2,1)S(1)}, u32[]{:S(2)}, u32[]{:S(2)}) async-start(bf16[2,128,3,512]{3,0,2,1:T(2,128)(2,1)} %copy.291), calls=%async_computation.1 | async-start | bytes 1572864 | tf_op jit(solution)/shard_map/all_to_all | solution.py:304
  113.4 1.7 convolution_convert_fusion.15
  115.1 1.5 copy.301
  116.6 3.8 %reshape.209 = bf16[1536,512]{1,0:T(8,128)(2,1)} reshape(bf16[512,1536]{1,0:T(8,128)(2,1)} %convolution_convert_fusion.2) | data formatting | bytes 3145728 | tf_op jit(solution)/shard_map/reshape | solution.py:308
  120.4 2.9 %convolution_convert_fusion.16 = bf16[512,512]{1,0:T(8,128)(2,1)} fusion(bf16[768,512]{1,0:T(8,128)(2,1)} %bitcast.221, bf16[64,8,6,128]{3,2,1,0:T(8,128)(2,1)} %bitcast.220), kind=kOutput, calls=%fused_computation.73 | convolution fusion | flops 402915328 | bytes 2097152 | tf_op jit(solution)/shard_map/dot_general | solution.py:64
  123.3 2.5 %fusion.22 = bf16[6,128,512]{2,1,0:T(8,128)(2,1)} fusion(f32[2,128,3,512]{3,1,2,0:T(8,128)S(1)} %copy-done.4, bf16[6,128,512]{1,2,0:T(8,128)(2,1)S(1)} %bitcast.207, bf16[512,512]{1,0:T(8,128)(2,1)} %param.17), kind=kOutput, calls=%fused_computation.45 | convolution fusion | flops 403439616 | bytes 3670016 | tf_op jit(solution)/shard_map/dot_general | solution.py:54
  128.2 2.9 %convolution_convert_fusion.12 = bf16[768,512]{1,0:T(8,128)(2,1)} fusion(bf16[768,512]{1,0:T(8,128)(2,1)S(1)} %reshape_reshape.15, bf16[512,512]{1,0:T(8,128)(2,1)} %param.15), kind=kOutput, calls=%fused_computation.66 | convolution fusion | flops 403046400 | bytes 2097152 | tf_op jit(solution)/shard_map/dot_general | solution.py:68
  131.1 1.4 copy.293
  135.5 2.7 %fusion.10 = (f32[8,8,96]{2,1,0:T(8,128)S(1)}, bf16[8,8,96,96]{2,3,1,0:T(8,128)(2,1)S(1)}) fusion(f32[8,8,96,96]{2,3,1,0:T(8,128)S(1)} %copy-done.6, f32[8,8,96]{2,1,0:T(8,128)S(1)} %multiply_divide_fusion, pred[96,96]{0,1:T(8,128)(4,1)S(1)} %iota_compare_fusion, bf16[8,96,1,8,64]{1,4,3,0,2:T(8,128)(2,1)} %copy.318, bf16[8,8,64,96]{3,0,2,1:T(8,128)(2,1)S(1)} %bitcast.210), kind=kOutput, calls=%fused_computation.18 | convolution fusion | flops 79620096 | bytes 5170176 | tf_op jit(solution)/shard_map/transpose(jvp(ghlm,gmhe->glhe))/dot_general | solution.py:40
  139.5 1.4 fusion.31
  143.2 4.5 %copy.299 = bf16[8,96,3,8,64]{1,0,4,3,2:T(8,128)(2,1)} copy(bf16[8,96,3,8,64]{1,4,3,0,2:T(8,128)(2,1)S(1)} %pad_add_fusion) | data formatting | bytes 4718592 | tf_op jit(solution)/shard_map/transpose(jvp())/add_any | solution.py:28
  147.7 6.2 %reshape.207 = bf16[768,1536]{0,1:T(8,128)(2,1)} reshape(bf16[8,96,3,8,64]{1,0,4,3,2:T(8,128)(2,1)} %copy.299) | data formatting | bytes 4718592 | tf_op jit(solution)/shard_map/reshape;transpose(jvp())/reshape | solution.py:73
  154.0 4.3 %convolution_convert_fusion.3 = bf16[512,1536]{1,0:T(8,128)(2,1)} fusion(bf16[768,512]{1,0:T(8,128)(2,1)S(1)} %bitcast.225, bf16[768,1536]{0,1:T(8,128)(2,1)} %reshape.207), kind=kOutput, calls=%fused_computation.25 | convolution fusion | flops 1208745984 | bytes 4718592 | tf_op jit(solution)/shard_map/dot_general | solution.py:74
  158.2 2.7 %reshape.208 = bf16[1536,512]{1,0:T(8,128)(2,1)S(1)} reshape(bf16[512,1536]{1,0:T(8,128)(2,1)} %convolution_convert_fusion.3) | data formatting | bytes 3145728 | tf_op jit(solution)/shard_map/reshape | solution.py:308
  162.3 67.5 %conditional.1 = (bf16[16384,128]{1,0:T(8,128)(2,1)}) conditional(s32[]{:T(128)} %bitcast.23, bf16[16384,128]{1,0:T(8,128)(2,1)S(1)} %bitcast.201, bf16[16384,128]{1,0:T(8,128)(2,1)S(1)} %bitcast.202), branch_computations={%region_7.8_spmd, %region_8.9_spmd} | conditional | bytes 8 | solution.py:261
  162.3 67.5 %branch_0_fun.1 = bf16[16384,128]{1,0:T(8,128)(2,1)} custom-call(bf16[16384,128]{1,0:T(8,128)(2,1)S(1)} %g_ref), custom_call_target="tpu_custom_call" | custom-call | tf_op jit(solution)/shard_map/cond/branch_0_fun/pallas_call | solution.py:236
  229.9 6.9 %convert_bitcast_fusion = f32[1,4096,512]{2,1,0:T(8,128)} fusion(bf16[512,4,8,128]{3,2,1,0:T(8,128)(2,1)} %bitcast.203), kind=kLoop, calls=%fused_computation | loop fusion | flops 2097152 | bytes 12582912 | tf_op jit(solution)/shard_map/convert_element_type | solution.py:313
  (88 shorter events, 24.3 us)
Async XLA Ops:
  0.6 67.6 %copy-start = (bf16[512,1536]{1,0:T(8,128)(2,1)S(1)}, bf16[512,1536]{1,0:T(8,128)(2,1)}, u32[]{:S(2)}) copy-start(bf16[512,1536]{1,0:T(8,128)(2,1)} %param.16) | copy-start | bytes 4718596
  32.3 2.6 %copy-start.5 = (f32[8,8,96,96]{2,3,1,0:T(8,128)}, f32[8,8,96,96]{2,3,1,0:T(8,128)S(1)}, u32[]{:S(2)}) copy-start(f32[8,8,96,96]{2,3,1,0:T(8,128)S(1)} %get-tuple-element.20) | copy-start | bytes 7077892
  32.3 2.0 copy-start.12
  32.3 2.6 %copy-start.25 = (bf16[512,512]{1,0:T(8,128)(2,1)S(1)}, bf16[512,512]{1,0:T(8,128)(2,1)}, u32[]{:S(2)}) copy-start(bf16[512,512]{1,0:T(8,128)(2,1)} %param.15) | copy-start | bytes 1572868
  34.3 1.2 copy-start.2
  34.8 1.0 copy-start.7
  35.5 12.2 %copy-start.19 = (bf16[2,128,3,512]{3,1,2,0:T(8,128)(2,1)S(1)}, bf16[2,128,3,512]{3,1,2,0:T(8,128)(2,1)}, u32[]{:S(2)}) copy-start(bf16[2,128,3,512]{3,1,2,0:T(8,128)(2,1)} %param.18) | copy-start | bytes 2359300
  37.3 23.9 %all-to-all-start = ((bf16[2,4,96,512]{3,1,0,2:T(4,128)(2,1)}), bf16[2,4,96,512]{3,1,0,2:T(4,128)(2,1)}, u32[]{:S(2)}, u32[]{:S(2)}) async-start(bf16[2,4,96,512]{3,1,0,2:T(4,128)(2,1)} %copy.266), calls=%async_computation | async-start | bytes 1572864 | tf_op jit(solution)/shard_map/all_to_all | solution.py:288
  47.0 6.6 %copy-start.8 = (bf16[8,8,64,96]{3,2,1,0:T(8,128)(2,1)S(1)}, bf16[8,8,64,96]{3,2,1,0:T(8,128)(2,1)}, u32[]{:S(2)}) copy-start(bf16[8,8,64,96]{3,2,1,0:T(8,128)(2,1)} %copy-done.7) | copy-start | bytes 2359300
  91.0 2.4 copy-start.15
  91.0 2.4 copy-start.18
  93.4 1.4 copy-start.17
  94.7 3.0 %copy-start.10 = (bf16[6,8,128,128]{2,3,1,0:T(8,128)(2,1)}, bf16[6,8,128,128]{2,3,1,0:T(8,128)(2,1)S(1)}, u32[]{:S(2)}) copy-start(bf16[6,8,128,128]{2,3,1,0:T(8,128)(2,1)S(1)} %get-tuple-element.14) | copy-start | bytes 4718596
  94.8 1.7 copy-start.16
  101.2 1.8 copy-start.20
  105.3 8.1 %copy-start.11 = (bf16[6,8,128,128]{2,3,1,0:T(8,128)(2,1)S(1)}, bf16[6,8,128,128]{2,3,1,0:T(8,128)(2,1)}, u32[]{:S(2)}) copy-start(bf16[6,8,128,128]{2,3,1,0:T(8,128)(2,1)} %copy-done.10) | copy-start | bytes 4718596
  108.1 19.0 %all-to-all-start.1 = ((bf16[2,128,3,512]{3,0,2,1:T(2,128)(2,1)}), bf16[2,128,3,512]{3,0,2,1:T(2,128)(2,1)S(1)}, u32[]{:S(2)}, u32[]{:S(2)}) async-start(bf16[2,128,3,512]{3,0,2,1:T(2,128)(2,1)} %copy.291), calls=%async_computation.1 | async-start | bytes 1572864 | tf_op jit(solution)/shard_map/all_to_all | solution.py:304
  116.6 6.7 %copy-start.4 = (f32[2,128,3,512]{3,1,2,0:T(8,128)S(1)}, f32[2,128,3,512]{3,1,2,0:T(8,128)}, u32[]{:S(2)}) copy-start(f32[2,128,3,512]{3,1,2,0:T(8,128)} %copy.270) | copy-start | bytes 4718596
  128.2 2.9 %copy-start.22 = (bf16[768,512]{1,0:T(8,128)(2,1)}, bf16[768,512]{1,0:T(8,128)(2,1)S(1)}, u32[]{:S(2)}) copy-start(bf16[768,512]{1,0:T(8,128)(2,1)S(1)} %reshape_reshape.15) | copy-start | bytes 2359300
  128.2 5.4 %copy-start.3 = (bf16[8,8,96,96]{2,3,1,0:T(8,128)(2,1)S(1)}, bf16[8,8,96,96]{2,3,1,0:T(8,128)(2,1)}, u32[]{:S(2)}) copy-start(bf16[8,8,96,96]{2,3,1,0:T(8,128)(2,1)} %copy-done.2) | copy-start | bytes 3538948
  133.6 1.9 copy-start.6
  135.5 2.7 %copy-start.14 = (bf16[8,96,1,8,64]{1,4,3,0,2:T(8,128)(2,1)S(1)}, bf16[8,96,1,8,64]{1,4,3,0,2:T(8,128)(2,1)}, u32[]{:S(2)}) copy-start(bf16[8,96,1,8,64]{1,4,3,0,2:T(8,128)(2,1)} %copy.320) | copy-start | bytes 2359300
  138.3 1.2 copy-start.13
  139.5 1.4 copy-start.21
  139.5 1.4 copy-start.23
  147.7 6.2 %copy-start.24 = (bf16[2,4,96,512]{3,2,1,0:T(8,128)(2,1)S(1)}, bf16[2,4,96,512]{3,2,1,0:T(8,128)(2,1)}, u32[]{:S(2)}) copy-start(bf16[2,4,96,512]{3,2,1,0:T(8,128)(2,1)} %get-tuple-element.17) | copy-start | bytes 2359300
  158.2 2.7 %copy-start.9 = (bf16[1536,512]{1,0:T(8,128)(2,1)S(1)}, bf16[1536,512]{1,0:T(8,128)(2,1)}, u32[]{:S(2)}) copy-start(bf16[1536,512]{1,0:T(8,128)(2,1)} %reshape.209) | copy-start | bytes 4718596
  229.9 6.9 %copy-start.1 = (bf16[512,1536]{1,0:T(8,128)(2,1)S(1)}, bf16[512,1536]{1,0:T(8,128)(2,1)}, u32[]{:S(2)}) copy-start(bf16[512,1536]{1,0:T(8,128)(2,1)} %param.16) | copy-start | bytes 4718596

commit v2 on v1

--- a/solution.py
+++ b/solution.py
@@ -8,88 +8,7 @@
 from jax.experimental.pallas import tpu as pltpu
 from jax.sharding import PartitionSpec as P
 
-HEADS = 8
-
-
 epsilon = 1e-05
-
-
-def normalize(hidden):
-    wide = hidden.astype(jnp.float32)
-    factor = lax.rsqrt(jnp.mean(wide * wide, axis=-1, keepdims=True) + epsilon)
-    return (wide * factor).astype(jnp.bfloat16)
-
-
-def attend(stacked_array, heads, causal):
-    groups, length, triple = stacked_array.shape
-    width = triple // 3
-    size = width // heads
-    parts = stacked_array.reshape(groups, length, 3, heads, size)
-    query = parts[:, :, 0]
-    keys = parts[:, :, 1]
-    values = parts[:, :, 2]
-    scores = jnp.einsum("glhe,gmhe->ghlm", query, keys, preferred_element_type=jnp.float32) * (
-        1.0 / math.sqrt(size)
-    )
-    powers = jnp.exp(scores)
-    if causal:
-        allowed = jnp.arange(length)[:, None] >= jnp.arange(length)[None, :]
-        powers = jnp.where(allowed, powers, 0.0)
-    shares = powers / jnp.sum(powers, axis=-1, keepdims=True)
-    rounded = shares.astype(jnp.bfloat16)
-    mixed_slope_estimate = jnp.einsum(
-        "ghlm,gmhe->glhe", rounded, values, preferred_element_type=jnp.float32
-    )
-    return mixed_slope_estimate.reshape(groups, length, width).astype(jnp.bfloat16)
-
-
-def sublayer_forward(hidden, w_qkv, w_out, heads, causal):
-    groups, length, width = hidden.shape
-    normed, norm_back = jax.vjp(normalize, hidden)
-    stacked_array = jnp.dot(normed.reshape(-1, width), w_qkv, preferred_element_type=jnp.float32)
-    stacked_array = stacked_array.astype(jnp.bfloat16).reshape(groups, length, 3 * width)
-    mixed_slope_estimate, attend_back = jax.vjp(
-        partial(attend, heads=heads, causal=causal), stacked_array
-    )
-    result = hidden.astype(jnp.float32) + jnp.dot(
-        mixed_slope_estimate.reshape(-1, width), w_out, preferred_element_type=jnp.float32
-    ).reshape(groups, length, width)
-    return (result, (normed, mixed_slope_estimate, norm_back, attend_back))
-
-
-def sublayer_backward(upstream, saved, w_qkv, w_out, need_input):
-    normed, mixed_slope_estimate, norm_back, attend_back = saved
-    groups, length, width = upstream.shape
-    flat_up = upstream.reshape(-1, width)
-    grad_out = jnp.dot(
-        mixed_slope_estimate.reshape(-1, width).T, flat_up, preferred_element_type=jnp.float32
-    )
-    grad_mixed = (
-        jnp.dot(flat_up, w_out.T, preferred_element_type=jnp.float32)
-        .astype(jnp.bfloat16)
-        .reshape(groups, length, width)
-    )
-    (grad_packed,) = attend_back(grad_mixed)
-    flat_packed = grad_packed.reshape(-1, 3 * width)
-    grad_qkv = jnp.dot(normed.reshape(-1, width).T, flat_packed, preferred_element_type=jnp.float32)
-    if not need_input:
-        return (grad_qkv, grad_out, None)
-    grad_normed = (
-        jnp.dot(flat_packed, w_qkv.T, preferred_element_type=jnp.float32)
-        .astype(jnp.bfloat16)
-        .reshape(groups, length, width)
-    )
-    (grad_hidden,) = norm_back(grad_normed)
-    combined = (grad_hidden.astype(jnp.float32) + upstream.astype(jnp.float32)).astype(jnp.bfloat16)
-    return (grad_qkv, grad_out, combined)
-
-
-def embed(rows, feeder_table):
-    table_rows = feeder_table.shape[0]
-    onehot = (rows[:, None] == jnp.arange(table_rows, dtype=jnp.int32)[None, :]).astype(
-        jnp.bfloat16
-    )
-    return jnp.dot(onehot, feeder_table, preferred_element_type=jnp.float32)
 
 
 MESH = pl.DeviceIdType.MESH
@@ -266,6 +185,236 @@
     )
 
 
+def exchange_kernel(count, send_ref, got_ref, send_sem, recv_sem, own_sem):
+    gossip = lax.axis_index("gossip")
+    me = lax.axis_index("field")
+    rows = send_ref.shape[0] // count
+
+    def block(i):
+        return pl.ds(pl.multiple_of(i * rows, 8), rows)
+
+    def peer(i):
+        return (gossip, lax.rem(me + i, count))
+
+    barrier = pltpu.get_barrier_semaphore()
+
+    def greet(i, carry):
+        pl.semaphore_signal(barrier, inc=1, device_id=peer(i), device_id_type=MESH)
+        return carry
+
+    lax.fori_loop(1, count, greet, 0)
+    own = pltpu.make_async_copy(send_ref.at[block(me)], got_ref.at[block(me)], own_sem)
+    own.start()
+    pl.semaphore_wait(barrier, count - 1)
+
+    def copy(i):
+        to = lax.rem(me + i, count)
+        return pltpu.make_async_remote_copy(
+            src_ref=send_ref.at[block(to)],
+            dst_ref=got_ref.at[block(me)],
+            send_sem=send_sem.at[i],
+            recv_sem=recv_sem.at[i],
+            device_id=(gossip, to),
+            device_id_type=MESH,
+        )
+
+    def start(i, carry):
+        copy(i).start()
+        return carry
+
+    def finish(i, carry):
+        copy(i).wait()
+        return carry
+
+    lax.fori_loop(1, count, start, 0)
+    lax.fori_loop(1, count, finish, 0)
+    own.wait()
+
+
+def exchange(blocks, count, collective_id):
+    return pl.pallas_call(
+        partial(exchange_kernel, count),
+        out_shape=jax.ShapeDtypeStruct(blocks.shape, blocks.dtype),
+        in_specs=[pl.BlockSpec(memory_space=pltpu.VMEM)],
+        out_specs=pl.BlockSpec(memory_space=pltpu.VMEM),
+        scratch_shapes=[
+            pltpu.SemaphoreType.DMA((count,)),
+            pltpu.SemaphoreType.DMA((count,)),
+            pltpu.SemaphoreType.DMA(()),
+        ],
+        compiler_params=pltpu.CompilerParams(collective_id=collective_id, has_side_effects=True),
+    )(blocks)
+
+
+SIZE = 64
+PAIR = 2 * SIZE
+
+
+def dot(a, b, contract=((1,), (0,))):
+    return lax.dot_general(a, b, (contract, ((), ())), preferred_element_type=jnp.float32)
+
+
+NT = ((1,), (1,))
+TN = ((0,), (0,))
+
+
+def first_lanes(rows):
+    return lax.broadcasted_iota(jnp.int32, (rows, PAIR), 1) < SIZE
+
+
+def stacked(pair):
+    low = first_lanes(pair.shape[0])
+    nothing = jnp.zeros_like(pair)
+    return jnp.concatenate([jnp.where(low, pair, nothing), jnp.where(low, nothing, pair)], axis=0)
+
+
+def unstacked(both):
+    rows = both.shape[0] // 2
+    return jnp.where(first_lanes(rows), both[:rows], both[rows:])
+
+
+def norm_factor(wide):
+    return lax.rsqrt(jnp.mean(wide * wide, axis=-1, keepdims=True) + epsilon)
+
+
+def weights_of(q, k, causal):
+    length = k.shape[0]
+    powers = jnp.exp(dot(stacked(q), k, NT) * (1.0 / math.sqrt(SIZE)))
+    if causal:
+        query = lax.broadcasted_iota(jnp.int32, powers.shape, 0) % length
+        key = lax.broadcasted_iota(jnp.int32, powers.shape, 1)
+        powers = jnp.where(query >= key, powers, 0.0)
+    return powers / jnp.sum(powers, axis=-1, keepdims=True)
+
+
+def attend_forward(packed, mixed, weights, sequences, length, causal):
+    width = mixed.shape[1]
+
+    def one(n, carry):
+        rows = pl.ds(pl.multiple_of(n * length, 16), length)
+        for p in range(width // PAIR):
+            lanes = p * PAIR
+            q = packed[rows, lanes : lanes + PAIR]
+            k = packed[rows, width + lanes : width + lanes + PAIR]
+            v = packed[rows, 2 * width + lanes : 2 * width + lanes + PAIR]
+            w = weights_of(q, k, causal).astype(jnp.bfloat16)
+            weights[n, p] = w
+            mixed[rows, lanes : lanes + PAIR] = unstacked(dot(w, v)).astype(jnp.bfloat16)
+        return carry
+
+    lax.fori_loop(0, sequences, one, 0)
+
+
+def attend_backward(packed, weights, d_mixed, d_packed, sequences, length):
+    width = d_mixed.shape[1]
+
+    def one(n, carry):
+        rows = pl.ds(pl.multiple_of(n * length, 16), length)
+        for p in range(width // PAIR):
+            lanes = p * PAIR
+            q = packed[rows, lanes : lanes + PAIR]
+            k = packed[rows, width + lanes : width + lanes + PAIR]
+            v = packed[rows, 2 * width + lanes : 2 * width + lanes + PAIR]
+            up = stacked(d_mixed[rows, lanes : lanes + PAIR])
+            w = weights[n, p]
+            wide = w.astype(jnp.float32)
+            d_w = dot(up, v, NT).astype(jnp.bfloat16).astype(jnp.float32)
+            d_scores = wide * (d_w - jnp.sum(d_w * wide, axis=-1, keepdims=True))
+            d_scores = (d_scores * (1.0 / math.sqrt(SIZE))).astype(jnp.bfloat16)
+            d_q = unstacked(dot(d_scores, k))
+            d_k = dot(d_scores, stacked(q), TN)
+            d_v = dot(w, up, TN)
+            d_packed[rows, lanes : lanes + PAIR] = d_q.astype(jnp.bfloat16)
+            d_packed[rows, width + lanes : width + lanes + PAIR] = d_k.astype(jnp.bfloat16)
+            d_packed[rows, 2 * width + lanes : 2 * width + lanes + PAIR] = d_v.astype(jnp.bfloat16)
+        return carry
+
+    lax.fori_loop(0, sequences, one, 0)
+
+
+def permuted(order, values):
+    rows = order.shape[0]
+    lane = lax.broadcasted_iota(jnp.int32, (rows, values.shape[0]), 1)
+    onehot = jnp.where(order == lane, 1.0, 0.0).astype(jnp.bfloat16)
+    return dot(onehot, values).astype(jnp.bfloat16)
+
+
+def time_forward_kernel(
+    batch, x_ref, row_ref, table_ref, qkv_ref, out_ref, order_ref, sent, normed, packed, weights, mixed, first
+):
+    sequences, length, width = x_ref.shape
+    feeders = sequences // batch
+    table_rows = table_ref.shape[0]
+    onehot = (row_ref[...] == lax.broadcasted_iota(jnp.int32, (row_ref.shape[0], table_rows), 1)).astype(jnp.bfloat16)
+    added = dot(onehot, table_ref[...])
+    for n in range(sequences):
+        rows = pl.ds(n * length, length)
+        start = x_ref[n].astype(jnp.float32) + added[n % feeders : n % feeders + 1]
+        first[rows, :] = start
+        normed[rows, :] = (start * norm_factor(start)).astype(jnp.bfloat16)
+    packed[...] = dot(normed[...], qkv_ref[...]).astype(jnp.bfloat16)
+    attend_forward(packed, mixed, weights, sequences, length, True)
+    result = (first[...] + dot(mixed[...], out_ref[...])).astype(jnp.bfloat16)
+    sent[...] = permuted(order_ref[...], result)
+
+
+def feed_kernel(
+    got_ref, order_ref, back_ref, adjoint_ref, qkv_ref, out_ref,
+    load, sent, grad_qkv, grad_out, hidden, normed, packed, weights, mixed, d_mixed, d_packed,
+):
+    sequences, length, width = load.shape
+    hidden[...] = permuted(order_ref[...], got_ref[...])
+    wide = hidden[...].astype(jnp.float32)
+    normed[...] = (wide * norm_factor(wide)).astype(jnp.bfloat16)
+    packed[...] = dot(normed[...], qkv_ref[...]).astype(jnp.bfloat16)
+    attend_forward(packed, mixed, weights, sequences, length, False)
+    result = hidden[...].astype(jnp.float32) + dot(mixed[...], out_ref[...])
+    load[...] = result.astype(jnp.bfloat16).reshape(load.shape)
+    up = adjoint_ref[...]
+    d_mixed[...] = dot(up, out_ref[...], NT).astype(jnp.bfloat16)
+    attend_backward(packed, weights, d_mixed, d_packed, sequences, length)
+    g = dot(d_packed[...], qkv_ref[...], NT).astype(jnp.bfloat16).astype(jnp.float32)
+    wide = hidden[...].astype(jnp.float32)
+    factor = norm_factor(wide)
+    along = jnp.sum(g * wide, axis=-1, keepdims=True) * (factor * factor * factor) * (1.0 / width)
+    d_hidden = (g * factor - wide * along).astype(jnp.bfloat16)
+    total = (d_hidden.astype(jnp.float32) + up.astype(jnp.float32)).astype(jnp.bfloat16)
+    sent[...] = permuted(back_ref[...], total)
+    grad_out[...] = dot(mixed[...], up, TN).astype(jnp.bfloat16)
+    for part in range(3):
+        lanes = slice(part * width, (part + 1) * width)
+        grad_qkv[part] = dot(normed[...], d_packed[:, lanes], TN).astype(jnp.bfloat16)
+
+
+def time_backward_kernel(
+    got_ref, order_ref, normed, packed, weights, mixed, out_ref, grad_qkv, grad_out, up, d_mixed, d_packed
+):
+    sequences = weights.shape[0]
+    length = weights.shape[3]
+    width = mixed.shape[1]
+    up[...] = permuted(order_ref[...], got_ref[...])
+    d_mixed[...] = dot(up[...], out_ref[...], NT).astype(jnp.bfloat16)
+    attend_backward(packed, weights, d_mixed, d_packed, sequences, length)
+    grad_out[...] = dot(mixed[...], up[...], TN).astype(jnp.bfloat16)
+    for part in range(3):
+        lanes = slice(part * width, (part + 1) * width)
+        grad_qkv[part] = dot(normed[...], d_packed[:, lanes], TN).astype(jnp.bfloat16)
+
+
+VMEM = pl.BlockSpec(memory_space=pltpu.VMEM)
+
+
+def call(kernel, outs, scratch, *args):
+    return pl.pallas_call(
+        kernel,
+        out_shape=tuple(jax.ShapeDtypeStruct(shape, jnp.bfloat16) for shape in outs),
+        in_specs=[VMEM] * len(args),
+        out_specs=tuple(VMEM for _ in outs),
+        scratch_shapes=[pltpu.VMEM(shape, held) for shape, held in scratch],
+        compiler_params=pltpu.CompilerParams(vmem_limit_bytes=48 << 20),
+    )(*args)
+
+
 def on_device(
     measured_features,
     feeder_of_row,
@@ -280,38 +429,94 @@
     batch, feed_local, slot_count, width = measured_features.shape
     feeder_count = adjoint_of_prediction.shape[1]
     slot_local = adjoint_of_prediction.shape[2]
-    added = embed(feeder_of_row, feeder_table)
-    start = measured_features.astype(jnp.float32) + added[None, :, None, :]
-    start = start.reshape(batch * feed_local, slot_count, width)
-    first, saved_time = sublayer_forward(start, time_qkv, time_out, HEADS, True)
-    first = first.astype(jnp.bfloat16).reshape(batch, feed_local, slot_count, width)
-    by_slot = lax.all_to_all(first, "field", split_axis=2, concat_axis=1, tiled=True)
-    regrouped = jnp.transpose(by_slot, (0, 2, 1, 3)).reshape(
-        batch * slot_local, feeder_count, width
-    )
-    right_factor, saved_feed = sublayer_forward(regrouped, feed_qkv, feed_out, HEADS, False)
-    right_factor = right_factor.astype(jnp.bfloat16).reshape(batch, slot_local, feeder_count, width)
-    predicted_load = jnp.transpose(right_factor, (0, 2, 1, 3))
-    upstream = jnp.transpose(adjoint_of_prediction, (0, 2, 1, 3)).reshape(
-        batch * slot_local, feeder_count, width
-    )
-    feeder_query_gradient, grad_fo, regrouped_gradient_rows = sublayer_backward(
-        upstream, saved_feed, feed_qkv, feed_out, True
-    )
-    grad_slots = jnp.transpose(
-        regrouped_gradient_rows.reshape(batch, slot_local, feeder_count, width), (0, 2, 1, 3)
-    )
-    grad_first = lax.all_to_all(grad_slots, "field", split_axis=1, concat_axis=2, tiled=True)
-    grad_first = grad_first.reshape(batch * feed_local, slot_count, width)
-    grad_tq, grad_to, unused = sublayer_backward(grad_first, saved_time, time_qkv, time_out, False)
-    local_grads = jnp.concatenate(
-        [grad_tq.reshape(-1, width), grad_to, feeder_query_gradient.reshape(-1, width), grad_fo],
-        axis=0,
-    )
-    tiles = local_grads.astype(jnp.bfloat16).reshape(512, 8, 4, LANES).transpose(0, 2, 1, 3).reshape(-1, LANES)
+    count = feeder_count // feed_local
+    rows = batch * feed_local * slot_count
+    pairs = width // PAIR
+    bf16 = jnp.bfloat16
+
+    at = jnp.arange(rows, dtype=jnp.int32)
+    wire = at.reshape(batch, feed_local, count, slot_local)
+    to_wire = wire.transpose(2, 3, 0, 1).reshape(rows, 1)
+    wired = at.reshape(count, slot_local, batch, feed_local)
+    from_wire = wired.transpose(2, 3, 0, 1).reshape(rows, 1)
+    feed = at.reshape(batch, slot_local, count, feed_local)
+    feed_to_wire = feed.transpose(2, 1, 0, 3).reshape(rows, 1)
+    wire_to_feed = wired.transpose(2, 1, 0, 3).reshape(rows, 1)
+
+    row_column = jnp.pad(feeder_of_row, (0, 8 - feed_local)).reshape(8, 1)
+    sequences = batch * feed_local
+    sent, normed, packed, weights, mixed = call(
+        partial(time_forward_kernel, batch),
+        (
+            (rows, width),
+            (rows, width),
+            (rows, 3 * width),
+            (sequences, pairs, 2 * slot_count, slot_count),
+            (rows, width),
+        ),
+        (((rows, width), jnp.float32),),
+        measured_features.reshape(sequences, slot_count, width),
+        row_column,
+        feeder_table,
+        time_qkv,
+        time_out,
+        to_wire,
+    )
+    got = exchange(sent, count, 3)
+    groups = batch * slot_local
+    upstream = jnp.transpose(adjoint_of_prediction, (0, 2, 1, 3)).reshape(rows, width)
+    load, back, feed_grad_qkv, feed_grad_out = call(
+        feed_kernel,
+        ((groups, feeder_count, width), (rows, width), (3, width, width), (width, width)),
+        (
+            ((rows, width), bf16),
+            ((rows, width), bf16),
+            ((rows, 3 * width), bf16),
+            ((groups, pairs, 2 * feeder_count, feeder_count), bf16),
+            ((rows, width), bf16),
+            ((rows, width), bf16),
+            ((rows, 3 * width), bf16),
+        ),
+        got,
+        wire_to_feed,
+        feed_to_wire,
+        upstream,
+        feed_qkv,
+        feed_out,
+    )
+    predicted_load = jnp.transpose(
+        load.reshape(batch, slot_local, feeder_count, width), (0, 2, 1, 3)
+    )
+    returned = exchange(back, count, 4)
+    time_grad_qkv, time_grad_out = call(
+        time_backward_kernel,
+        ((3, width, width), (width, width)),
+        (
+            ((rows, width), bf16),
+            ((rows, width), bf16),
+            ((rows, 3 * width), bf16),
+        ),
+        returned,
+        from_wire,
+        normed,
+        packed,
+        weights,
+        mixed,
+        time_out,
+    )
+    parts = [time_grad_qkv, time_grad_out[None], feed_grad_qkv, feed_grad_out[None]]
+    local_grads = jnp.concatenate(parts, axis=0).reshape(-1, width)
+    tiles = local_grads.reshape(512, 8, 4, LANES).transpose(0, 2, 1, 3).reshape(-1, LANES)
     mean = pair_mean(tiles, round_index)
-    mean = mean.reshape(512, 4, 8, LANES).transpose(0, 2, 1, 3).reshape(4096, 512).astype(jnp.float32)
-    return (predicted_load, mean[None])
+    mean = mean.reshape(512, 4, 8, LANES).transpose(0, 2, 1, 3).reshape(8, width, width)
+    mean = mean.astype(jnp.float32)
+    pieces = [
+        mean[0:3].transpose(1, 0, 2).reshape(-1, width),
+        mean[3],
+        mean[4:7].transpose(1, 0, 2).reshape(-1, width),
+        mean[7],
+    ]
+    return (predicted_load, jnp.concatenate(pieces, axis=0)[None])
 
 
 def solution(mesh):

time: 239 us -> 204 us (0.85); the launches traced: 237 us -> 207 us
  Pallas kernels: 67.5 us -> 155 us
  matrix products: 47.8 us -> 0 us
  local copies, waits for them, and re-layouts: 82.1 us -> 41.2 us
  starting transfers between devices: 15 us -> 0 us
  other arithmetic: 18 us -> 9.55 us
  waiting for transfers between devices: 4.39 us -> 0 us
    pallas_call x0 -> x5, Pallas kernels: none -> 87.5 us  [the longest x3 47.1 us: call(): pl.pallas_call(kernel, out_shape=tuple((jax.ShapeDtypeStruct(shape, jnp.b...]
    dot_general x24 -> x0, matrix products: 47.8 us -> none  [the longest x6 9.8 us: attend(): jnp.einsum('glhe,gmhe->ghlm', query, keys, preferred_element_type=jnp.flo...]
    all_to_all x2 -> x0, starting transfers between devices: 15 us -> none  [the longest x1 9.66 us: on_device(): lax.all_to_all(first, 'field', split_axis=2, concat_axis=1, tiled=True)]
    another operation x3 -> x0, local copies, waits for them, and re-layouts: 14.6 us -> none  [the longest x2 13.9 us: attend(): parts = stacked_array.reshape(groups, length, 3, heads, size)]
    convert_element_type x8 -> x0, local copies, waits for them, and re-layouts: 12.5 us -> none  [the longest x3 5.96 us: attend(): mixed_slope_estimate.reshape(groups, length, width).astype(jnp.bfloat16)]
    convert_element_type x6 -> x1, other arithmetic: 13 us -> 3.38 us  [on_device(): mean = mean.astype(jnp.float32)]
    transpose x1 -> x2, local copies, waits for them, and re-layouts: 1.71 us -> 10.2 us  [the longest x1 6.06 us: on_device(): mean[0:3].transpose(1, 0, 2).reshape(-1, width)]
    slice x2 -> x1, local copies, waits for them, and re-layouts: 9.24 us -> 2.35 us  [on_device(): mean[0:3].transpose(1, 0, 2).reshape(-1, width)]
  transfers between devices with their start and end apart: 2 -> 0, of which waited for: 2 -> 0; matrix products, arithmetic and copies ran while one was open for 10% -> 0% of each run, Pallas kernels for 0% -> 0%
where the time goes in v2:
time: 204 us; the launch traced here: 207 us
  Pallas kernels  155 us (76%)
  local copies, waits for them, and re-layouts  41.2 us (20%)
  other arithmetic  9.55 us (5%)
    pallas_call x1, Pallas kernels, run(): pl.pallas_call(partial(reduce_kernel, tuple(chains), used), out_shape=jax...  67 us
    pallas_call x3, Pallas kernels, call(): pl.pallas_call(kernel, out_shape=tuple((jax.ShapeDtypeStruct(shape, jnp.b...  47.1 us
    pallas_call x2, Pallas kernels, exchange(): pl.pallas_call(partial(exchange_kernel, count), out_shape=jax.ShapeDtypeS...  40.4 us
    unnamed x34, local copies, waits for them, and re-layouts  15.3 us
    transpose x1, local copies, waits for them, and re-layouts, on_device(): mean[0:3].transpose(1, 0, 2).reshape(-1, width)  6.06 us
    reshape x1, local copies, waits for them, and re-layouts, on_device(): mean[0:3].transpose(1, 0, 2).reshape(-1, width)  5.93 us
    broadcast_in_dim x1, other arithmetic, on_device(): return (predicted_load, jnp.concatenate(pieces, axis=0)[None])  5.5 us
    reshape x1, local copies, waits for them, and re-layouts, on_device(): mean[4:7].transpose(1, 0, 2).reshape(-1, width)  4.48 us

profile of v2, /device:TPU:0, one launch (start us, length us, event | category | flops | bytes accessed | tf_op | source)
XLA Modules:
  0.0 207.2 jit_solution(5535014867121489297)
XLA Ops:
  1.3 0.7 pad_bitcast_fusion
  1.9 0.1 copy.12.row_ref
  2.1 0.1 reshape.425.order_ref
  2.3 0.2 reshape.424.back_ref
  2.5 0.1 reshape.423.order_ref
  2.6 0.2 reshape.422.order_ref
  2.8 0.0 copy-start.2
  2.8 1.0 copy-done.2
  3.9 0.0 copy-start.11
  3.9 1.1 copy-done.11
  5.0 0.0 copy-start.16
  5.0 0.9 copy-done.16
  5.9 9.7 %shard_map.104 = (bf16[768,512]{1,0:T(8,128)(2,1)S(1)}, bf16[768,512]{1,0:T(8,128)(2,1)S(1)}, bf16[768,1536]{1,0:T(8,128)(2,1)}, bf16[8,4,192,96]{3,2,1,0:T(8,128)(2,1)S(1)}, bf16[768,512]{1,0:T(8,128)(2,1)S(1)}) custom-call(bf16[8,96,512]{2,1,0:T(8,128)(2,1)S(1)} %bitcast.37, s32[8,1]{1,0:T(8,128)S(1)} %copy.12.row_ref, bf16[128,512]{1,0:T(8,128)(2,1)S(1)} %copy-done.16, ...), custom_call_target="tpu_custom_call" | custom-call | tf_op jit(solution)/shard_map/pallas_call | solution.py:408
  15.6 0.0 copy-start.4
  15.6 1.2 copy-done.4
  16.8 0.0 copy-start.5
  16.8 0.9 copy-done.5
  17.6 0.0 copy-start.7
  17.6 0.9 copy-done.7
  18.5 0.9 copy-done.9
  19.4 22.2 %shard_map.105.got_ref = bf16[768,512]{1,0:T(8,128)(2,1)} custom-call(bf16[768,512]{1,0:T(8,128)(2,1)} %copy-done.9), custom_call_target="tpu_custom_call" | custom-call | tf_op jit(solution)/shard_map/pallas_call | solution.py:235
  41.6 0.0 copy-start.1
  41.7 1.1 copy-done.1
  42.8 1.1 copy-done.12
  43.9 1.0 copy-done.13
  45.0 21.3 %shard_map.106 = (bf16[6,128,512]{2,1,0:T(8,128)(2,1)}, bf16[768,512]{1,0:T(8,128)(2,1)S(1)}, bf16[3,512,512]{2,1,0:T(8,128)(2,1)S(1)}, bf16[512,512]{1,0:T(8,128)(2,1)S(1)}) custom-call(bf16[768,512]{1,0:T(8,128)(2,1)S(1)} %copy-done.1, s32[768,1]{1,0:T(8,128)S(1)} %reshape.423.order_ref, s32[768,1]{1,0:T(8,128)S(1)} %reshape.424.back_ref, ...), custom_call_target="tpu_custom_call" | custom-call | tf_op jit(solution)/shard_map/pallas_call | solution.py:408
  66.3 0.0 copy-start.10
  66.3 0.9 copy-done.10
  67.2 0.8 copy-done.14
  68.0 18.2 %shard_map.107.got_ref = bf16[768,512]{1,0:T(8,128)(2,1)} custom-call(bf16[768,512]{1,0:T(8,128)(2,1)} %copy-done.10), custom_call_target="tpu_custom_call" | custom-call | tf_op jit(solution)/shard_map/pallas_call | solution.py:235
  86.2 0.0 copy-done.3
  86.2 0.0 copy-start
  86.2 1.1 copy-done
  87.3 1.1 copy-done.6
  88.4 1.1 copy-done.8
  89.6 16.1 %shard_map.108 = (bf16[3,512,512]{2,1,0:T(8,128)(2,1)S(1)}, bf16[512,512]{1,0:T(8,128)(2,1)S(1)}) custom-call(bf16[768,512]{1,0:T(8,128)(2,1)S(1)} %copy-done, s32[768,1]{1,0:T(8,128)S(1)} %reshape.425.order_ref, bf16[768,512]{1,0:T(8,128)(2,1)S(1)} %copy-done.6, bf16[768,1536]{1,0:T(8,128)(2,1)} %get-tuple-element.22.packed, ...), custom_call_target="tpu_custom_call" | custom-call | tf_op jit(solution)/shard_map/pallas_call | solution.py:408
  105.7 0.0 copy-done.15
  105.7 0.6 pad_maximum_fusion
  106.3 67.4 %conditional.1 = (bf16[16384,128]{1,0:T(8,128)(2,1)}) conditional(s32[]{:T(128)} %bitcast.6, bf16[16384,128]{1,0:T(8,128)(2,1)S(1)} %bitcast.41, bf16[16384,128]{1,0:T(8,128)(2,1)S(1)} %bitcast.42), branch_computations={%region_0.1_spmd, %region_1.2_spmd} | conditional | bytes 8 | solution.py:180
  106.5 67.0 %branch_0_fun.1 = bf16[16384,128]{1,0:T(8,128)(2,1)} custom-call(bf16[16384,128]{1,0:T(8,128)(2,1)S(1)} %g_ref), custom_call_target="tpu_custom_call" | custom-call | tf_op jit(solution)/shard_map/cond/branch_0_fun/pallas_call | solution.py:155
  173.7 3.4 %convert_bitcast_fusion = f32[512,8,4,128]{3,1,2,0:T(8,128)S(1)} fusion(bf16[512,4,8,128]{3,2,1,0:T(8,128)(2,1)} %bitcast.43), kind=kLoop, calls=%fused_computation.1 | loop fusion | flops 2097152 | bytes 12582912 | tf_op jit(solution)/shard_map/convert_element_type | solution.py:512
  177.1 1.5 slice_bitcast_fusion.1
  178.7 2.4 %fusion.1 = (f32[192,8,4,128]{3,1,2,0:T(8,128)}, f32[192,8,4,128]{3,1,2,0:T(8,128)S(1)}) fusion(f32[512,8,4,128]{3,1,2,0:T(8,128)S(1)} %convert_bitcast_fusion), kind=kLoop, calls=%fused_computation.11 | loop fusion | bytes 12582912 | tf_op jit(solution)/shard_map/slice | solution.py:514
  181.0 4.2 %copy.18 = f32[512,3,512]{2,1,0:T(4,128)} copy(f32[512,3,512]{2,0,1:T(8,128)S(1)} %bitcast.45) | data formatting | bytes 6291456 | tf_op jit(solution)/shard_map/transpose | solution.py:516
  185.2 4.5 %reshape.419 = f32[1536,512]{1,0:T(8,128)S(1)} reshape(f32[512,3,512]{2,1,0:T(4,128)} %copy.18) | data formatting | bytes 6291456 | tf_op jit(solution)/shard_map/reshape | solution.py:516
  189.7 6.1 %copy.17 = f32[512,3,512]{2,1,0:T(4,128)} copy(f32[512,3,512]{2,0,1:T(8,128)} %bitcast.44) | data formatting | bytes 6291456 | tf_op jit(solution)/shard_map/transpose | solution.py:514
  195.7 5.9 %reshape.418 = f32[1536,512]{1,0:T(8,128)} reshape(f32[512,3,512]{2,1,0:T(4,128)} %copy.17) | data formatting | bytes 6291456 | tf_op jit(solution)/shard_map/reshape | solution.py:514
  201.7 5.5 %maximum_bitcast_fusion = f32[1,4096,512]{2,1,0:T(8,128)} fusion(f32[512,512]{1,0:T(8,128)} %get-tuple-element.32, f32[1536,512]{1,0:T(8,128)S(1)} %reshape.419, f32[512,512]{1,0:T(8,128)} %get-tuple-element.31, f32[1536,512]{1,0:T(8,128)} %reshape.418), kind=kLoop, calls=%fused_computation | loop fusion | flops 6291456 | bytes 16777216 | tf_op jit(solution)/shard_map/broadcast_in_dim | solution.py:519
  (12 shorter events, 0.1 us)
Async XLA Ops:
  2.8 1.0 copy-start.2
  3.9 1.1 copy-start.11
  5.0 0.9 copy-start.16
  15.6 1.2 copy-start.4
  16.8 0.9 copy-start.5
  17.6 0.9 copy-start.7
  18.5 0.9 copy-start.9
  19.4 66.8 %copy-start.3 = (bf16[512,512]{1,0:T(8,128)(2,1)S(1)}, bf16[512,512]{1,0:T(8,128)(2,1)}, u32[]{:S(2)}) copy-start(bf16[512,512]{1,0:T(8,128)(2,1)} %out_ref.5) | copy-start | bytes 1572868
  41.6 1.1 copy-start.1
  42.8 1.1 copy-start.12
  43.9 1.0 copy-start.13
  66.3 0.9 copy-start.10
  67.2 0.8 copy-start.14
  68.0 37.7 %copy-start.15 = (bf16[512,512]{1,0:T(8,128)(2,1)S(1)}, bf16[512,512]{1,0:T(8,128)(2,1)}, u32[]{:S(2)}) copy-start(bf16[512,512]{1,0:T(8,128)(2,1)} %copy-done.14) | copy-start | bytes 1572868
  86.2 1.1 copy-start
  87.3 1.1 copy-start.6
  88.4 1.1 copy-start.8

commit v3 on v2

--- a/solution.py
+++ b/solution.py
@@ -339,6 +339,17 @@
     return dot(onehot, values).astype(jnp.bfloat16)
 
 
+def store_gradients(grads, normed, d_packed, mixed, up):
+    slabs, parts, width, lanes = grads.shape
+    for part in range(parts):
+        if part < 3:
+            total = dot(normed[...], d_packed[:, part * width : (part + 1) * width], TN)
+        else:
+            total = dot(mixed[...], up, TN)
+        for slab in range(slabs):
+            grads[slab, part] = total[:, slab * lanes : (slab + 1) * lanes].astype(jnp.bfloat16)
+
+
 def time_forward_kernel(
     batch, x_ref, row_ref, table_ref, qkv_ref, out_ref, order_ref, sent, normed, packed, weights, mixed, first
 ):
@@ -360,7 +371,7 @@
 
 def feed_kernel(
     got_ref, order_ref, back_ref, adjoint_ref, qkv_ref, out_ref,
-    load, sent, grad_qkv, grad_out, hidden, normed, packed, weights, mixed, d_mixed, d_packed,
+    load, sent, grads, hidden, normed, packed, weights, mixed, d_mixed, d_packed,
 ):
     sequences, length, width = load.shape
     hidden[...] = permuted(order_ref[...], got_ref[...])
@@ -380,14 +391,11 @@
     d_hidden = (g * factor - wide * along).astype(jnp.bfloat16)
     total = (d_hidden.astype(jnp.float32) + up.astype(jnp.float32)).astype(jnp.bfloat16)
     sent[...] = permuted(back_ref[...], total)
-    grad_out[...] = dot(mixed[...], up, TN).astype(jnp.bfloat16)
-    for part in range(3):
-        lanes = slice(part * width, (part + 1) * width)
-        grad_qkv[part] = dot(normed[...], d_packed[:, lanes], TN).astype(jnp.bfloat16)
+    store_gradients(grads, normed, d_packed, mixed, up)
 
 
 def time_backward_kernel(
-    got_ref, order_ref, normed, packed, weights, mixed, out_ref, grad_qkv, grad_out, up, d_mixed, d_packed
+    got_ref, order_ref, normed, packed, weights, mixed, out_ref, grads, up, d_mixed, d_packed
 ):
     sequences = weights.shape[0]
     length = weights.shape[3]
@@ -395,10 +403,41 @@
     up[...] = permuted(order_ref[...], got_ref[...])
     d_mixed[...] = dot(up[...], out_ref[...], NT).astype(jnp.bfloat16)
     attend_backward(packed, weights, d_mixed, d_packed, sequences, length)
-    grad_out[...] = dot(mixed[...], up[...], TN).astype(jnp.bfloat16)
-    for part in range(3):
-        lanes = slice(part * width, (part + 1) * width)
-        grad_qkv[part] = dot(normed[...], d_packed[:, lanes], TN).astype(jnp.bfloat16)
+    store_gradients(grads, normed, d_packed, mixed, up[...])
+
+
+def finish_kernel(mean_ref, out_ref, wide, sem):
+    layers, slabs, parts, depth, lanes = mean_ref.shape
+    rows = parts * depth
+    copies = []
+    for layer in range(layers):
+        for slab in range(slabs):
+            target = wide.at[layer * slabs + slab]
+            columns = pl.ds(slab * lanes, lanes)
+            for part in range(3):
+                target[pl.ds(part, depth, stride=3), :] = mean_ref[layer, slab, part].astype(jnp.float32)
+            target[3 * depth :, :] = mean_ref[layer, slab, 3].astype(jnp.float32)
+            copies.append(
+                pltpu.make_async_copy(
+                    target, out_ref.at[pl.ds(layer * rows, rows), columns], sem.at[layer * slabs + slab]
+                )
+            )
+            copies[-1].start()
+    for copy in copies:
+        copy.wait()
+
+
+def finished(mean):
+    layers, slabs, parts, depth, lanes = mean.shape
+    shape = (layers * parts * depth, slabs * lanes)
+    return pl.pallas_call(
+        finish_kernel,
+        out_shape=jax.ShapeDtypeStruct(shape, jnp.float32),
+        in_specs=[pl.BlockSpec(memory_space=pltpu.VMEM)],
+        out_specs=pl.BlockSpec(memory_space=pl.ANY),
+        scratch_shapes=[pltpu.VMEM((layers * slabs, parts * depth, lanes), jnp.float32), pltpu.SemaphoreType.DMA((layers * slabs,))],
+        compiler_params=pltpu.CompilerParams(vmem_limit_bytes=32 << 20),
+    )(mean)
 
 
 VMEM = pl.BlockSpec(memory_space=pltpu.VMEM)
@@ -462,12 +501,13 @@
         time_out,
         to_wire,
     )
+    slabs = (width // LANES, 4, width, LANES)
     got = exchange(sent, count, 3)
     groups = batch * slot_local
     upstream = jnp.transpose(adjoint_of_prediction, (0, 2, 1, 3)).reshape(rows, width)
-    load, back, feed_grad_qkv, feed_grad_out = call(
+    load, back, feed_grads = call(
         feed_kernel,
-        ((groups, feeder_count, width), (rows, width), (3, width, width), (width, width)),
+        ((groups, feeder_count, width), (rows, width), slabs),
         (
             ((rows, width), bf16),
             ((rows, width), bf16),
@@ -488,9 +528,9 @@
         load.reshape(batch, slot_local, feeder_count, width), (0, 2, 1, 3)
     )
     returned = exchange(back, count, 4)
-    time_grad_qkv, time_grad_out = call(
+    (time_grads,) = call(
         time_backward_kernel,
-        ((3, width, width), (width, width)),
+        (slabs,),
         (
             ((rows, width), bf16),
             ((rows, width), bf16),
@@ -504,19 +544,9 @@
         mixed,
         time_out,
     )
-    parts = [time_grad_qkv, time_grad_out[None], feed_grad_qkv, feed_grad_out[None]]
-    local_grads = jnp.concatenate(parts, axis=0).reshape(-1, width)
-    tiles = local_grads.reshape(512, 8, 4, LANES).transpose(0, 2, 1, 3).reshape(-1, LANES)
-    mean = pair_mean(tiles, round_index)
-    mean = mean.reshape(512, 4, 8, LANES).transpose(0, 2, 1, 3).reshape(8, width, width)
-    mean = mean.astype(jnp.float32)
-    pieces = [
-        mean[0:3].transpose(1, 0, 2).reshape(-1, width),
-        mean[3],
-        mean[4:7].transpose(1, 0, 2).reshape(-1, width),
-        mean[7],
-    ]
-    return (predicted_load, jnp.concatenate(pieces, axis=0)[None])
+    grads = jnp.stack([time_grads, feed_grads])
+    mean = pair_mean(grads.reshape(-1, LANES), round_index).reshape(grads.shape)
+    return (predicted_load, finished(mean)[None])
 
 
 def solution(mesh):

time: 204 us -> 182 us (0.89); the launches traced: 207 us -> 181 us
  local copies, waits for them, and re-layouts: 41.2 us -> 16.1 us
  other arithmetic: 9.55 us -> 2.06 us
  Pallas kernels: 155 us -> 161 us
    reshape x2 -> x0, local copies, waits for them, and re-layouts: 10.4 us -> none  [the longest x1 5.93 us: on_device(): mean[0:3].transpose(1, 0, 2).reshape(-1, width)]
    transpose x2 -> x0, local copies, waits for them, and re-layouts: 10.2 us -> none  [the longest x1 6.06 us: on_device(): mean[0:3].transpose(1, 0, 2).reshape(-1, width)]
    pallas_call x0 -> x1, Pallas kernels: none -> 5.62 us  [finished(): pl.pallas_call(finish_kernel, out_shape=jax.ShapeDtypeStruct(shape, jnp.f...]
    broadcast_in_dim x1 -> x0, other arithmetic: 5.5 us -> none  [on_device(): return (predicted_load, jnp.concatenate(pieces, axis=0)[None])]
    convert_element_type x1 -> x0, other arithmetic: 3.38 us -> none  [on_device(): mean = mean.astype(jnp.float32)]
    slice x1 -> x0, local copies, waits for them, and re-layouts: 2.35 us -> none  [on_device(): mean[0:3].transpose(1, 0, 2).reshape(-1, width)]
    unnamed x34 -> x32, local copies, waits for them, and re-layouts: 15.3 us -> 14.7 us
where the time goes in v3:
time: 182 us; the launch traced here: 181 us
  Pallas kernels  161 us (88%)
  local copies, waits for them, and re-layouts  16.1 us (9%)
  other arithmetic  2.06 us (1%)
    pallas_call x1, Pallas kernels, run(): pl.pallas_call(partial(reduce_kernel, tuple(chains), used), out_shape=jax...  66.9 us
    pallas_call x3, Pallas kernels, call(): pl.pallas_call(kernel, out_shape=tuple((jax.ShapeDtypeStruct(shape, jnp.b...  48.1 us
    pallas_call x2, Pallas kernels, exchange(): pl.pallas_call(partial(exchange_kernel, count), out_shape=jax.ShapeDtypeS...  40.3 us
    unnamed x32, local copies, waits for them, and re-layouts  14.7 us
    pallas_call x1, Pallas kernels, finished(): pl.pallas_call(finish_kernel, out_shape=jax.ShapeDtypeStruct(shape, jnp.f...  5.62 us

profile of v3, /device:TPU:0, one launch (start us, length us, event | category | flops | bytes accessed | tf_op | source)
XLA Modules:
  0.0 181.2 jit_solution(8224688391254738160)
XLA Ops:
  1.3 0.7 pad_bitcast_fusion
  1.9 0.1 copy.12.row_ref
  2.1 0.1 reshape.409.order_ref
  2.3 0.2 reshape.408.back_ref
  2.5 0.1 reshape.407.order_ref
  2.6 0.2 reshape.406.order_ref
  2.8 0.0 copy-start.2
  2.8 1.0 copy-done.2
  3.9 0.0 copy-start.11
  3.9 1.1 copy-done.11
  5.0 0.0 copy-start.14
  5.0 0.9 copy-done.14
  5.9 9.7 %shard_map.104 = (bf16[768,512]{1,0:T(8,128)(2,1)S(1)}, bf16[768,512]{1,0:T(8,128)(2,1)S(1)}, bf16[768,1536]{1,0:T(8,128)(2,1)}, bf16[8,4,192,96]{3,2,1,0:T(8,128)(2,1)S(1)}, bf16[768,512]{1,0:T(8,128)(2,1)S(1)}) custom-call(bf16[8,96,512]{2,1,0:T(8,128)(2,1)S(1)} %bitcast.19, s32[8,1]{1,0:T(8,128)S(1)} %copy.12.row_ref, bf16[128,512]{1,0:T(8,128)(2,1)S(1)} %copy-done.14, ...), custom_call_target="tpu_custom_call" | custom-call | tf_op jit(solution)/shard_map/pallas_call | solution.py:447
  15.6 0.0 copy-start.5
  15.6 0.9 copy-done.5
  16.5 0.0 copy-start.7
  16.5 0.9 copy-done.7
  17.4 0.0 copy-start.9
  17.4 0.9 copy-done.9
  18.2 0.0 copy-start.3
  18.2 22.2 %shard_map.105.got_ref = bf16[768,512]{1,0:T(8,128)(2,1)} custom-call(bf16[768,512]{1,0:T(8,128)(2,1)} %copy-done.9), custom_call_target="tpu_custom_call" | custom-call | tf_op jit(solution)/shard_map/pallas_call | solution.py:235
  40.5 0.0 copy-start.1
  40.5 1.1 copy-done.1
  41.6 0.0 copy-start.4
  41.6 1.4 copy-done.4
  43.0 0.0 copy-start.12
  43.0 1.1 copy-done.12
  44.1 0.0 copy-start.13
  44.1 1.0 copy-done.13
  45.2 21.2 %shard_map.106 = (bf16[6,128,512]{2,1,0:T(8,128)(2,1)}, bf16[768,512]{1,0:T(8,128)(2,1)S(1)}, bf16[4,4,512,128]{3,2,1,0:T(8,128)(2,1)}) custom-call(bf16[768,512]{1,0:T(8,128)(2,1)S(1)} %copy-done.1, s32[768,1]{1,0:T(8,128)S(1)} %reshape.407.order_ref, s32[768,1]{1,0:T(8,128)S(1)} %reshape.408.back_ref, bf16[768,512]{1,0:T(8,128)(2,1)S(1)} %bitcast.20, ...), custom_call_target="tpu_custom_call" | custom-call | tf_op jit(solution)/shard_map/pallas_call | solution.py:447
  66.4 0.0 copy-start.10
  66.4 0.9 copy-done.10
  67.3 18.1 %shard_map.107.got_ref = bf16[768,512]{1,0:T(8,128)(2,1)} custom-call(bf16[768,512]{1,0:T(8,128)(2,1)} %copy-done.10), custom_call_target="tpu_custom_call" | custom-call | tf_op jit(solution)/shard_map/pallas_call | solution.py:235
  85.5 0.0 copy-done.3
  85.5 0.0 copy-start
  85.5 1.1 copy-done
  86.6 0.0 copy-start.6
  86.6 1.1 copy-done.6
  87.7 0.0 copy-start.8
  87.7 1.1 copy-done.8
  88.9 0.0 copy-start.15
  88.9 17.2 %shard_map.108 = bf16[4,4,512,128]{3,2,1,0:T(8,128)(2,1)} custom-call(bf16[768,512]{1,0:T(8,128)(2,1)S(1)} %copy-done, s32[768,1]{1,0:T(8,128)S(1)} %reshape.409.order_ref, bf16[768,512]{1,0:T(8,128)(2,1)S(1)} %copy-done.6, bf16[768,1536]{1,0:T(8,128)(2,1)} %get-tuple-element.19.packed, bf16[8,4,192,96]{3,2,1,0:T(8,128)(2,1)S(1)} %get-tuple-element.20.weights, ...), custom_call_target="tpu_custom_call" | custom-call | tf_op jit(solution)/shard_map/pallas_call | solution.py:447
  106.0 0.0 copy-done.15
  106.0 2.0 %pad_maximum_fusion = bf16[2,4,4,512,128]{4,3,2,1,0:T(8,128)(2,1)S(1)} fusion(bf16[1,4,4,512,128]{4,3,2,1,0:T(8,128)(2,1)S(1)} %bitcast.26, bf16[1,4,4,512,128]{4,3,2,1,0:T(8,128)(2,1)} %bitcast.25), kind=kLoop, calls=%fused_computation | loop fusion | flops 2097152 | bytes 8388608 | tf_op jit(solution)/shard_map/stack | solution.py:547
  108.0 67.4 %conditional.1 = (bf16[16384,128]{1,0:T(8,128)(2,1)}) conditional(s32[]{:T(128)} %bitcast.6, bf16[16384,128]{1,0:T(8,128)(2,1)S(1)} %bitcast.21, bf16[16384,128]{1,0:T(8,128)(2,1)S(1)} %bitcast.22), branch_computations={%region_0.1_spmd, %region_1.2_spmd} | conditional | bytes 8 | solution.py:180
  108.2 66.9 %branch_0_fun.1 = bf16[16384,128]{1,0:T(8,128)(2,1)} custom-call(bf16[16384,128]{1,0:T(8,128)(2,1)S(1)} %g_ref), custom_call_target="tpu_custom_call" | custom-call | tf_op jit(solution)/shard_map/cond/branch_0_fun/pallas_call | solution.py:155
  175.4 5.6 %shard_map.109 = f32[4096,512]{1,0:T(8,128)} custom-call(bf16[2,4,4,512,128]{4,3,2,1,0:T(8,128)(2,1)} %bitcast.23), custom_call_target="tpu_custom_call" | custom-call | tf_op jit(solution)/shard_map/pallas_call | solution.py:433
  (4 shorter events, 0.1 us)
Async XLA Ops:
  2.8 1.0 copy-start.2
  3.9 1.1 copy-start.11
  5.0 0.9 copy-start.14
  15.6 0.9 copy-start.5
  16.5 0.9 copy-start.7
  17.4 0.9 copy-start.9
  18.2 67.2 %copy-start.3 = (bf16[512,512]{1,0:T(8,128)(2,1)S(1)}, bf16[512,512]{1,0:T(8,128)(2,1)}, u32[]{:S(2)}) copy-start(bf16[512,512]{1,0:T(8,128)(2,1)} %out_ref.5) | copy-start | bytes 1572868
  40.5 1.1 copy-start.1
  41.6 1.4 copy-start.4
  43.0 1.1 copy-start.12
  44.1 1.0 copy-start.13
  66.4 0.9 copy-start.10
  85.5 1.1 copy-start
  86.6 1.1 copy-start.6
  87.7 1.1 copy-start.8
  88.9 17.2 %copy-start.15 = (bf16[4,4,512,128]{3,2,1,0:T(8,128)(2,1)S(1)}, bf16[4,4,512,128]{3,2,1,0:T(8,128)(2,1)}, u32[]{:S(2)}) copy-start(bf16[4,4,512,128]{3,2,1,0:T(8,128)(2,1)} %get-tuple-element.22) | copy-start | bytes 6291460
